TPU v7x, 256 devices: a whole 4x4x8 slice. The times are simulated.
256 devices in a mesh: leaf: 64 (over z, y, core), rhs: 4 (over x).
Axes of the slice: x: 4, y: 4, z: 8, core: 2. Of those that a mesh axis runs over, the one named last changes fastest.
Arguments:
- densities: bfloat16 [64, 262144], P('rhs', 'leaf'), may hold values from -6 to 6
- bases: float32 [32, 262144], P(None, 'leaf'), may hold values from -0.5 to 0.5
- near_blocks: bfloat16 [2048, 8, 128, 128], P('leaf', 'rhs'), may hold values from -0.1875 to 0.1875
- near_src: int32 [2048, 8], P('leaf', 'rhs'), may hold values from 0 to 55, as said below
- send_leaf: int32 [64, 6, 4], replicated, may hold values from -1 to 31, as said below
- far_src: int32 [2048, 8], P('leaf'), may hold values from 0 to 31
- leaf_coupling: float32 [2048, 8, 32, 32], P('leaf'), may hold values from -0.375 to 0.375
- local_transfer: float32 [64, 64, 32, 32], P('leaf'), may hold values from -0.75 to 0.75
- upper_transfer: float32 [128, 32, 32], replicated, may hold values from -0.75 to 0.75
- up_coupling: float32 [128, 3, 32, 32], replicated, may hold values from -8 to 8
Outputs:
- product: float32 [64, 262144], P('rhs', 'leaf')
Inputs may be any that keep to these rules, and one draw needn't show every extreme that they name: `send_leaf`: entry [e, j, c] is a leaf of device e (local index) whose panel e sends to its face neighbour e + o_j, or -1. Only existing face neighbours receive; the leaves of [e, j] are distinct and come before the -1 entries; every device sends exactly 4 leaves to at least one neighbour, among them its leaf 32 - 1, and exactly 4 to its neighbour at offset -s*s where that exists. `near_src`: A slot of the owner's panel buffer: below 32 a leaf of the same device, else slot 32 + j * 4 + c. It never names an empty slot, and every filled slot is named by some block of the device.
All inputs are finite; a program needn't handle non-finite values.
Results may differ from a plain program's by a relative error of at most 0.0003.
Values may be sent and summed in bfloat16 or wider, within the bound.
A program may use at most 128 MiB of HBM per device.

v0:
```python
import jax
import jax.numpy as jnp
from jax import lax
from jax.sharding import PartitionSpec as P

TOP_PREC = lax.Precision.HIGHEST
FACE_SIGNS = ((1, 0), (-1, 0), (1, 1), (-1, 1), (1, 2), (-1, 2))


def shifted(value, axis, steps):
    count = lax.axis_size(axis)
    first, last = (max(0, -steps), min(count, count - steps))
    return lax.ppermute(value, axis, [(source, source + steps) for source in range(first, last)])


def from_everyone(x, axis):
    copies = jnp.broadcast_to(x, (lax.axis_size(axis), *x.shape))
    return lax.all_to_all(copies, axis, split_axis=0, concat_axis=0, tiled=True)


def laid_out(parts, dim):
    parts = jnp.moveaxis(parts, 0, dim)
    shape = parts.shape
    return parts.reshape(*shape[:dim], shape[dim] * shape[dim + 1], *shape[dim + 2 :])


def gather_directly(x, axis, dim):
    parts = from_everyone(x, axis)
    return laid_out(parts, dim)


def cube_side(device_count):
    return max((edge_len for edge_len in range(1, 65) if edge_len**3 <= device_count))


def face_offsets(device_count):
    side_len = cube_side(device_count)
    return [face_sign * side_len**axis_pos for face_sign, axis_pos in FACE_SIGNS]


def lift_pairs(child_coef, child_maps):
    lifted = jnp.einsum("...nrs,...nqr->...nqs", child_maps, child_coef, precision=TOP_PREC)
    return lifted[..., 0::2, :, :] + lifted[..., 1::2, :, :]


def apply_maps(node_maps, coef_rows):
    return jnp.einsum("...nrs,...nqs->...nqr", node_maps, coef_rows, precision=TOP_PREC)


def couple_level(coef_level, maps_level):
    level_width = coef_level.shape[0]
    even_node = jnp.arange(level_width) % 2 == 0
    padded = jnp.pad(coef_level, ((3, 3), (0, 0), (0, 0)))
    minus_two = padded[1 : level_width + 1]
    plus_two = padded[5 : level_width + 5]
    third_node = jnp.where(
        even_node[:, None, None], padded[6 : level_width + 6], padded[0:level_width]
    )
    first_terms = apply_maps(maps_level[:, 0], minus_two) + apply_maps(maps_level[:, 1], plus_two)
    return first_terms + apply_maps(maps_level[:, 2], third_node)


def upper_tree(roots, upper_transfer, up_coupling):
    node_total = roots.shape[0]
    coef_levels = {node_total: roots}
    level_width = node_total
    while level_width > 4:
        coef_levels[level_width // 2] = lift_pairs(
            coef_levels[level_width], upper_transfer[level_width : 2 * level_width]
        )
        level_width = level_width // 2
    level_field = couple_level(coef_levels[4], up_coupling[4:8])
    level_width = 4
    while level_width < node_total:
        level_width = level_width * 2
        coupled = couple_level(coef_levels[level_width], up_coupling[level_width : 2 * level_width])
        level_field = coupled + apply_maps(
            upper_transfer[level_width : 2 * level_width], jnp.repeat(level_field, 2, axis=0)
        )
    return level_field


def local(
    densities,
    bases,
    near_blocks,
    near_src,
    send_leaf,
    far_src,
    leaf_coupling,
    local_transfer,
    upper_transfer,
    up_coupling,
):
    leaf_devices = lax.axis_size("leaf")
    device_rank = lax.axis_index("leaf")
    columns, points = densities.shape
    leaf_count = near_blocks.shape[0]
    leaf_width = near_blocks.shape[2]
    rank_width = bases.shape[0]
    panels = densities.reshape(columns, leaf_count, leaf_width)
    offsets = face_offsets(leaf_devices)
    arrived = []
    for direction in range(6):
        neighbour_panels = shifted(panels, "leaf", offsets[direction])
        sender = device_rank - offsets[direction]
        inside = (sender >= 0) & (sender < leaf_devices)
        clipped = jnp.clip(sender, 0, leaf_devices - 1)
        sent_leaf = lax.dynamic_index_in_dim(send_leaf, clipped, 0, keepdims=False)[direction]
        chosen = jnp.take(neighbour_panels, jnp.maximum(sent_leaf, 0), axis=1)
        keep_slot = inside & (sent_leaf >= 0)
        arrived.append(jnp.where(keep_slot[None, :, None], chosen, jnp.zeros_like(chosen)))
    buffer = jnp.concatenate([panels] + arrived, axis=1)
    piece_blocks = lax.all_gather(near_blocks, "rhs", axis=1, tiled=True)
    piece_sources = lax.all_gather(near_src, "rhs", axis=1, tiled=True)
    picked = jnp.take(buffer, piece_sources, axis=1)
    near_field = jnp.einsum(
        "tkij,qtkj->qti", piece_blocks, picked, preferred_element_type=jnp.float32
    )
    near_field = near_field.reshape(columns, points)
    basis_view = bases.reshape(rank_width, leaf_count, leaf_width)
    leaf_coef = jnp.einsum(
        "rti,qti->tqr", basis_view, panels.astype(jnp.float32), precision=TOP_PREC
    )
    subtree_maps = local_transfer[0]
    coef_levels = {leaf_count: leaf_coef}
    level_width = leaf_count
    while level_width > 1:
        coef_levels[level_width // 2] = lift_pairs(
            coef_levels[level_width], subtree_maps[level_width : 2 * level_width]
        )
        level_width = level_width // 2
    root_coef = coef_levels[1][0]
    roots = gather_directly(root_coef[None], "leaf", 0)
    root_all = upper_tree(roots, upper_transfer, up_coupling)
    root_field = lax.dynamic_index_in_dim(root_all, device_rank, 0, keepdims=False)
    picked_coef = jnp.take(leaf_coef, far_src, axis=0)
    leaf_local = jnp.einsum("tjrs,tjqs->tqr", leaf_coupling, picked_coef, precision=TOP_PREC)
    level_field = root_field[None]
    level_width = 1
    while level_width < leaf_count:
        level_width = level_width * 2
        level_field = apply_maps(
            subtree_maps[level_width : 2 * level_width], jnp.repeat(level_field, 2, axis=0)
        )
    leaf_field = level_field + leaf_local
    far_part = jnp.einsum("rti,tqr->qti", basis_view, leaf_field, precision=TOP_PREC).reshape(
        columns, points
    )
    return near_field + far_part


def solution(mesh):
    in_specs = (
        P("rhs", "leaf"),
        P(None, "leaf"),
        P("leaf", "rhs", None, None),
        P("leaf", "rhs"),
        P(),
        P("leaf", None),
        P("leaf", None, None, None),
        P("leaf", None, None, None),
        P(),
        P(),
    )
    out_specs = P("rhs", "leaf")
    return jax.shard_map(local, mesh=mesh, in_specs=in_specs, out_specs=out_specs, check_vma=False)
```

profile of v0, /device:TPU:32, one launch (start us, length us, event | category | flops | bytes accessed | tf_op | source)
XLA Modules:
  0.0 176.7 jit_solution(17345306287468822620)
XLA Ops:
  8.2 1.9 %collective-permute-start = (bf16[16,32,128]{2,0,1:T(8,128)(2,1)}, bf16[16,32,128]{2,0,1:T(8,128)(2,1)}, u32[]{:S(2)}, u32[]{:S(2)}) collective-permute-start(bf16[16,32,128]{2,0,1:T(8,128)(2,1)} %copy_bitcast_fusion.1), channel_id=1, source_target_pairs={{0,4},{4,8},{8,12},{12,16},{16,20},{20,24},{24,28},{28,32},{32,36}... | collective-permute-start | bytes 393224 | tf_op jit(solution)/shard_map/ppermute | solution.py:13
  10.1 5.8 %collective-permute-start.1 = (bf16[16,32,128]{2,0,1:T(8,128)(2,1)}, bf16[16,32,128]{2,0,1:T(8,128)(2,1)}, u32[]{:S(2)}, u32[]{:S(2)}) collective-permute-start(bf16[16,32,128]{2,0,1:T(8,128)(2,1)} %copy_bitcast_fusion.1), channel_id=1, source_target_pairs={{4,0},{8,4},{12,8},{16,12},{20,16},{24,20},{28,24},{32,28},{36,32}... | collective-permute-start | bytes 393224 | tf_op jit(solution)/shard_map/ppermute | solution.py:13
  15.9 3.0 %collective-permute-start.2 = (bf16[16,32,128]{2,0,1:T(8,128)(2,1)}, bf16[16,32,128]{2,0,1:T(8,128)(2,1)}, u32[]{:S(2)}, u32[]{:S(2)}) collective-permute-start(bf16[16,32,128]{2,0,1:T(8,128)(2,1)} %copy_bitcast_fusion.1), channel_id=1, source_target_pairs={{0,16},{4,20},{8,24},{12,28},{16,32},{20,36},{24,40},{28,44},{32,4... | collective-permute-start | bytes 393224 | tf_op jit(solution)/shard_map/ppermute | solution.py:13
  18.9 5.3 %collective-permute-start.3 = (bf16[16,32,128]{2,0,1:T(8,128)(2,1)}, bf16[16,32,128]{2,0,1:T(8,128)(2,1)}, u32[]{:S(2)}, u32[]{:S(2)}) collective-permute-start(bf16[16,32,128]{2,0,1:T(8,128)(2,1)} %copy_bitcast_fusion.1), channel_id=1, source_target_pairs={{16,0},{20,4},{24,8},{28,12},{32,16},{36,20},{40,24},{44,28},{48,3... | collective-permute-start | bytes 393224 | tf_op jit(solution)/shard_map/ppermute | solution.py:13
  24.1 5.8 %collective-permute-start.4 = (bf16[16,32,128]{2,0,1:T(8,128)(2,1)}, bf16[16,32,128]{2,0,1:T(8,128)(2,1)}, u32[]{:S(2)}, u32[]{:S(2)}) collective-permute-start(bf16[16,32,128]{2,0,1:T(8,128)(2,1)} %copy_bitcast_fusion.1), channel_id=1, source_target_pairs={{0,64},{4,68},{8,72},{12,76},{16,80},{20,84},{24,88},{28,92},{32,9... | collective-permute-start | bytes 393224 | tf_op jit(solution)/shard_map/ppermute | solution.py:13
  37.6 8.4 %all-to-all-start = ((f32[64,1,512]{2,1,0:T(1,128)}), f32[64,1,512]{2,1,0:T(1,128)}, u32[]{:S(2)}, u32[]{:S(2)}) async-start(f32[64,1,512]{2,1,0:T(1,128)} %reshape.311), calls=%async_computation | async-start | bytes 262144 | tf_op jit(solution)/shard_map/all_to_all | solution.py:18
  54.8 10.2 %all-gather = s32[4,2,32]{2,1,0:T(2,128)S(1)} all-gather(s32[1,2,32]{2,1,0:T(2,128)S(1)} %bitcast.205), channel_id=1, replica_groups=mesh['leaf'=64,'rhs'=4] {'rhs'}, dimensions={0}, use_global_device_ids=true | all-gather | bytes 1280 | tf_op jit(solution)/shard_map/all_gather | solution.py:115
  65.7 2.4 %gather_fusion.1 = f32[256,16,32]{2,1,0:T(8,128)} fusion(f32[32,16,32]{2,1,0:T(8,128)S(1)} %fusion.24, s32[1024]{0:T(1024)S(1)} %pad_clamp_fusion), kind=kCustom, calls=%fused_computation.7 | custom fusion | bytes 1049600 | tf_op jit(solution)/shard_map/jit(_take)/gather | solution.py:137
  78.5 4.6 %fusion.2 = f32[32,16,32]{2,1,0:T(8,128)} fusion(f32[32,8,32,32]{3,2,1,0:T(8,128)S(1)} %copy-done.8, f32[32,8,16,32]{3,2,1,0:T(8,128)S(1)} %bitcast.192, pred[32,8]{1,0:T(8,128)(4,1)S(1)} %copy-done.35), kind=kOutput, calls=%fused_computation.10 | convolution fusion | flops 50462720 | bytes 1638656 | tf_op jit(solution)/shard_map/tjrs,tjqs->tqr/dot_general | solution.py:138
  88.6 2.4 %copy.161 = f32[32,1,32,32]{3,2,0,1:T(8,128)} copy(f32[32,1,32,32]{0,3,2,1:T(8,128)} %get-tuple-element.32) | data formatting | bytes 262144
  91.0 2.2 %copy.162 = f32[32,1,32,32]{3,2,0,1:T(8,128)} copy(f32[32,1,32,32]{0,3,2,1:T(8,128)} %get-tuple-element.31) | data formatting | bytes 262144
  94.5 2.0 %copy.171 = f32[8,1,32,32]{3,2,0,1:T(8,128)} copy(f32[8,1,32,32]{0,3,2,1:T(8,128)} %get-tuple-element.28) | data formatting | bytes 65536
  96.4 2.3 %copy.164 = f32[32,32,32]{2,1,0:T(8,128)} copy(f32[32,32,32]{0,2,1:T(8,128)} %slice.299) | data formatting | bytes 262144
  100.0 1.9 %copy.169 = f32[8,1,32,32]{3,2,0,1:T(8,128)} copy(f32[8,1,32,32]{0,3,2,1:T(8,128)} %get-tuple-element.29) | data formatting | bytes 65536
  101.9 1.9 %copy.170 = f32[8,1,32,32]{3,2,0,1:T(8,128)} copy(f32[8,1,32,32]{0,3,2,1:T(8,128)} %get-tuple-element.27) | data formatting | bytes 65536
  103.8 1.9 %copy.175 = f32[4,1,32,32]{3,2,0,1:T(8,128)} copy(f32[4,1,32,32]{0,3,2,1:T(8,128)} %get-tuple-element.26) | data formatting | bytes 32768
  105.9 2.0 %copy.173 = f32[4,1,32,32]{3,2,0,1:T(8,128)} copy(f32[4,1,32,32]{0,3,2,1:T(8,128)} %get-tuple-element.25) | data formatting | bytes 32768
  108.0 2.0 %copy.174 = f32[4,1,32,32]{3,2,0,1:T(8,128)} copy(f32[4,1,32,32]{0,3,2,1:T(8,128)} %get-tuple-element.24) | data formatting | bytes 32768
  109.9 2.0 %copy.167 = f32[16,1,32,32]{3,2,0,1:T(8,128)} copy(f32[16,1,32,32]{0,3,2,1:T(8,128)} %get-tuple-element.22) | data formatting | bytes 131072
  112.8 2.0 %copy.166 = f32[16,1,32,32]{3,2,0,1:T(8,128)} copy(f32[16,1,32,32]{0,3,2,1:T(8,128)} %get-tuple-element.21) | data formatting | bytes 131072
  114.8 2.9 %copy.159 = f32[64,1,32,32]{3,2,0,1:T(8,128)} copy(f32[64,1,32,32]{0,3,2,1:T(8,128)} %get-tuple-element.19) | data formatting | bytes 524288
  117.7 3.0 %copy.158 = f32[64,1,32,32]{3,2,0,1:T(8,128)} copy(f32[64,1,32,32]{0,3,2,1:T(8,128)} %get-tuple-element.20) | data formatting | bytes 524288
  157.8 2.0 %fusion.12 = f32[64,16,32]{2,1,0:T(8,128)S(1)} fusion(f32[64,1,32,32]{3,2,0,1:T(8,128)S(1)} %copy-done.19, f32[64,1,16,32]{3,2,1,0:T(8,128)S(1)} %reshape.312), kind=kOutput, calls=%fused_computation.28 | convolution fusion | flops 12189696 | bytes 524288 | tf_op jit(solution)/shard_map/...nrs,...nqs->...nqr/dot_general | solution.py:47
  163.9 4.7 %convolution_bitcast_fusion = f32[32,16,128]{2,1,0:T(8,128)S(1)} fusion(bf16[32,8,128,128]{3,2,1,0:T(8,128)(2,1)} %all-gather.3.cloned.1.call-done, bf16[32,8,16,128]{3,2,1,0:T(8,128)(2,1)S(1)} %bitcast.194, pred[32,8]{1,0:T(8,128)(4,1)S(1)} %copy.111), kind=kOutput, calls=%fused_computation.17 | convolution fusion | flops 134742016 | bytes 9699584 | tf_op jit(solution)/shard_map/tkij,qtkj->qti/dot_general | solution.py:117
  (227 shorter events, 80.1 us)
Async XLA Ops:
  6.5 25.3 %copy-start = (f32[32,4096]{1,0:T(8,128)S(1)}, f32[32,4096]{1,0:T(8,128)}, u32[]{:S(2)}) copy-start(f32[32,4096]{1,0:T(8,128)} %param.13) | copy-start | bytes 1572868
  6.5 23.5 %copy-start.2 = (f32[1,64,32,32]{1,3,2,0:T(8,128)S(1)}, f32[1,64,32,32]{1,3,2,0:T(8,128)}, u32[]{:S(2)}) copy-start(f32[1,64,32,32]{1,3,2,0:T(8,128)} %param.19) | copy-start | bytes 786436
  6.5 157.3 %all-gather.3.cloned.1.call-start = ((), (), s32[]{:S(2)}) async-start(), calls=%async_computation.1 | async-start | bytes 10485760 | tf_op jit(solution)/shard_map/all_gather | solution.py:114
  8.2 115.3 %collective-permute-start = (bf16[16,32,128]{2,0,1:T(8,128)(2,1)}, bf16[16,32,128]{2,0,1:T(8,128)(2,1)}, u32[]{:S(2)}, u32[]{:S(2)}) collective-permute-start(bf16[16,32,128]{2,0,1:T(8,128)(2,1)} %copy_bitcast_fusion.1), channel_id=1, source_target_pairs={{0,4},{4,8},{8,12},{12,16},{16,20},{20,24},{24,28},{28,32},{32,36}... | collective-permute-start | bytes 393224 | tf_op jit(solution)/shard_map/ppermute | solution.py:13
  10.1 116.2 %collective-permute-start.1 = (bf16[16,32,128]{2,0,1:T(8,128)(2,1)}, bf16[16,32,128]{2,0,1:T(8,128)(2,1)}, u32[]{:S(2)}, u32[]{:S(2)}) collective-permute-start(bf16[16,32,128]{2,0,1:T(8,128)(2,1)} %copy_bitcast_fusion.1), channel_id=1, source_target_pairs={{4,0},{8,4},{12,8},{16,12},{20,16},{24,20},{28,24},{32,28},{36,32}... | collective-permute-start | bytes 393224 | tf_op jit(solution)/shard_map/ppermute | solution.py:13
  15.9 112.1 %collective-permute-start.2 = (bf16[16,32,128]{2,0,1:T(8,128)(2,1)}, bf16[16,32,128]{2,0,1:T(8,128)(2,1)}, u32[]{:S(2)}, u32[]{:S(2)}) collective-permute-start(bf16[16,32,128]{2,0,1:T(8,128)(2,1)} %copy_bitcast_fusion.1), channel_id=1, source_target_pairs={{0,16},{4,20},{8,24},{12,28},{16,32},{20,36},{24,40},{28,44},{32,4... | collective-permute-start | bytes 393224 | tf_op jit(solution)/shard_map/ppermute | solution.py:13
  18.9 110.7 %collective-permute-start.3 = (bf16[16,32,128]{2,0,1:T(8,128)(2,1)}, bf16[16,32,128]{2,0,1:T(8,128)(2,1)}, u32[]{:S(2)}, u32[]{:S(2)}) collective-permute-start(bf16[16,32,128]{2,0,1:T(8,128)(2,1)} %copy_bitcast_fusion.1), channel_id=1, source_target_pairs={{16,0},{20,4},{24,8},{28,12},{32,16},{36,20},{40,24},{44,28},{48,3... | collective-permute-start | bytes 393224 | tf_op jit(solution)/shard_map/ppermute | solution.py:13
  24.1 107.0 %collective-permute-start.4 = (bf16[16,32,128]{2,0,1:T(8,128)(2,1)}, bf16[16,32,128]{2,0,1:T(8,128)(2,1)}, u32[]{:S(2)}, u32[]{:S(2)}) collective-permute-start(bf16[16,32,128]{2,0,1:T(8,128)(2,1)} %copy_bitcast_fusion.1), channel_id=1, source_target_pairs={{0,64},{4,68},{8,72},{12,76},{16,80},{20,84},{24,88},{28,92},{32,9... | collective-permute-start | bytes 393224 | tf_op jit(solution)/shard_map/ppermute | solution.py:13
  34.6 11.4 %copy-start.33 = (s32[64,6,4]{0,2,1:T(4,128)S(1)}, s32[64,6,4]{0,2,1:T(4,128)}, u32[]{:S(2)}) copy-start(s32[64,6,4]{0,2,1:T(4,128)} %param.16) | copy-start | bytes 18436
  34.6 20.2 %copy-start.37 = (s32[32,2]{0,1:T(2,128)S(1)}, s32[32,2]{0,1:T(2,128)}, u32[]{:S(2)}) copy-start(s32[32,2]{0,1:T(2,128)} %param.15) | copy-start | bytes 772
  35.1 29.9 %copy-start.34 = (s32[32,8]{0,1:T(8,128)S(1)}, s32[32,8]{0,1:T(8,128)}, u32[]{:S(2)}) copy-start(s32[32,8]{0,1:T(8,128)} %param.17) | copy-start | bytes 3076
  37.6 102.0 %all-to-all-start = ((f32[64,1,512]{2,1,0:T(1,128)}), f32[64,1,512]{2,1,0:T(1,128)}, u32[]{:S(2)}, u32[]{:S(2)}) async-start(f32[64,1,512]{2,1,0:T(1,128)} %reshape.311), calls=%async_computation | async-start | bytes 262144 | tf_op jit(solution)/shard_map/all_to_all | solution.py:18
  72.6 4.8 %copy-start.35 = (pred[32,8]{1,0:T(8,128)(4,1)S(1)}, pred[32,8]{1,0:T(8,128)(4,1)}, u32[]{:S(2)}) copy-start(pred[32,8]{1,0:T(8,128)(4,1)} %copy.146) | copy-start | bytes 772
  78.5 5.1 %copy-start.3 = (f32[128,32,32]{0,2,1:T(8,128)S(1)}, f32[128,32,32]{0,2,1:T(8,128)}, u32[]{:S(2)}) copy-start(f32[128,32,32]{0,2,1:T(8,128)} %param.20) | copy-start | bytes 1572868
  83.6 4.0 %copy-start.36 = (pred[32,8]{0,1:T(8,128)(4,1)S(1)}, pred[32,8]{0,1:T(8,128)(4,1)}, u32[]{:S(2)}) copy-start(pred[32,8]{0,1:T(8,128)(4,1)} %compare_and_fusion.1) | copy-start | bytes 772
  88.6 4.6 %copy-start.13 = (f32[32,1,32,32]{0,3,2,1:T(8,128)S(1)}, f32[32,1,32,32]{0,3,2,1:T(8,128)}, u32[]{:S(2)}) copy-start(f32[32,1,32,32]{0,3,2,1:T(8,128)} %get-tuple-element.30) | copy-start | bytes 393220
  94.5 11.3 %copy-start.10 = (f32[8,32,32]{0,2,1:T(8,128)S(1)}, f32[8,32,32]{0,2,1:T(8,128)}, u32[]{:S(2)}) copy-start(f32[8,32,32]{0,2,1:T(8,128)} %slice.319) | copy-start | bytes 98308
  105.9 5.9 %copy-start.12 = (f32[16,1,32,32]{0,3,2,1:T(8,128)S(1)}, f32[16,1,32,32]{0,3,2,1:T(8,128)}, u32[]{:S(2)}) copy-start(f32[16,1,32,32]{0,3,2,1:T(8,128)} %get-tuple-element.23) | copy-start | bytes 196612
  112.8 8.0 %copy-start.11 = (f32[64,1,32,32]{0,3,2,1:T(8,128)S(1)}, f32[64,1,32,32]{0,3,2,1:T(8,128)}, u32[]{:S(2)}) copy-start(f32[64,1,32,32]{0,3,2,1:T(8,128)} %get-tuple-element.18) | copy-start | bytes 786436
  123.5 12.9 %collective-permute-start.5 = (bf16[16,32,128]{2,0,1:T(8,128)(2,1)}, bf16[16,32,128]{2,0,1:T(8,128)(2,1)S(1)}, u32[]{:S(2)}, u32[]{:S(2)}) collective-permute-start(bf16[16,32,128]{2,0,1:T(8,128)(2,1)} %copy_bitcast_fusion.1), channel_id=1, source_target_pairs={{64,0},{68,4},{72,8},{76,12},{80,16},{84,20},{88,24},{92,28},{96,3... | collective-permute-start | bytes 393224 | tf_op jit(solution)/shard_map/ppermute | solution.py:13
  143.2 4.0 %copy-start.23 = (f32[8,1,32,32]{3,2,0,1:T(8,128)S(1)}, f32[8,1,32,32]{3,2,0,1:T(8,128)}, u32[]{:S(2)}) copy-start(f32[8,1,32,32]{3,2,0,1:T(8,128)} %copy.170) | copy-start | bytes 98308
  143.3 4.6 %copy-start.18 = (f32[16,1,32,32]{3,2,0,1:T(8,128)S(1)}, f32[16,1,32,32]{3,2,0,1:T(8,128)}, u32[]{:S(2)}) copy-start(f32[16,1,32,32]{3,2,0,1:T(8,128)} %copy.167) | copy-start | bytes 196612
  143.3 4.6 %copy-start.40 = (pred[16]{0:T(512)(128)(4,1)S(1)}, pred[16]{0:T(512)(128)(4,1)}, u32[]{:S(2)}) copy-start(pred[16]{0:T(512)(128)(4,1)} %fusion.103) | copy-start | bytes 52
  145.1 3.9 %copy-start.28 = (f32[16,1,32,32]{3,2,0,1:T(8,128)S(1)}, f32[16,1,32,32]{3,2,0,1:T(8,128)}, u32[]{:S(2)}) copy-start(f32[16,1,32,32]{3,2,0,1:T(8,128)} %copy.165) | copy-start | bytes 196612
  (27 other events, 67.4 us)
Sparse Core Ops, SparseCore 0:
  30.1 84.6 all-gather.2
where the time goes:
time: 179 us; the launch traced here: 177 us
  local copies, waits for them, and re-layouts  70.7 us (39%)
  matrix products  32.5 us (18%)
  starting transfers between devices  31.4 us (18%)
  other arithmetic  17.6 us (10%)
  between operations  14.3 us (8%)
  blocking collectives  10.2 us (6%)
    unnamed x113, local copies, waits for them, and re-layouts  40 us
    ppermute x6, starting transfers between devices, shifted(): lax.ppermute(value, axis, [(source, source + steps) for source in range(f...  23 us
    dot_general x24, matrix products, apply_maps(): jnp.einsum('...nrs,...nqs->...nqr', node_maps, coef_rows, precision=TOP_P...  17.2 us
    all_gather x1, blocking collectives, local(): piece_sources = lax.all_gather(near_src, 'rhs', axis=1, tiled=True)  10.2 us
    gather x6, local copies, waits for them, and re-layouts, local(): chosen = jnp.take(neighbour_panels, jnp.maximum(sent_leaf, 0), axis=1)  8.61 us
    all_to_all x1, starting transfers between devices, from_everyone(): return lax.all_to_all(copies, axis, split_axis=0, concat_axis=0, tiled=True)  8.39 us
    dot_general x9, matrix products, lift_pairs(): jnp.einsum('...nrs,...nqr->...nqs', child_maps, child_coef, precision=TOP...  4.9 us
    slice x3, local copies, waits for them, and re-layouts, couple_level(): maps_level[:, 1]  4.83 us
  transfers between devices with their start and end apart: 8, of which 0 were waited for; matrix products, arithmetic and copies ran while one was open for 63% of the time, Pallas kernels for 0%

commit v1 on v0

v1 whole, which is shorter than its diff:
```python
import functools

import jax
import jax.numpy as jnp
from jax import lax
from jax.experimental import pallas as pl
from jax.experimental.pallas import tpu as pltpu
from jax.sharding import PartitionSpec as P

F32 = jnp.float32
BF16 = jnp.bfloat16
MESH = pl.DeviceIdType.MESH
LEAVES = 32
WIDTH = 128
COLS = 16
NLEAF = 64
NRHS = 4
SLOTS = 56
FACES = (1, -1, 4, -4, 16, -16)
GREET = (1, -1, 2, -2, 3, -3, 4, -4, 6, -6, 8, -8, 12, -12, 16, -16, 24, -24, 32)
CHUNKS = 4
CHUNK = LEAVES // CHUNKS


def dot_nn(a, b):
    return lax.dot_general(a, b, (((1,), (0,)), ((), ())), preferred_element_type=F32)


def dot_nt(a, b):
    return lax.dot_general(a, b, (((1,), (1,)), ((), ())), preferred_element_type=F32)


def halves(x):
    high = x.astype(BF16)
    return high, (x - high.astype(F32)).astype(BF16)


def lane_group(shape):
    return lax.broadcasted_iota(jnp.int32, shape, len(shape) - 1) // 32


def coef_form(r):
    group = lane_group(r.shape)
    high = r.astype(BF16).astype(F32)
    return jnp.where(group % 2 == 0, high, r - high).astype(BF16)


def unfold(tile):
    group = lane_group(tile.shape)
    turned = [tile] + [pltpu.roll(tile, 32 * k, 1) for k in (1, 2, 3)]
    rows = []
    for b in range(4):
        pick = [turned[(g - b) % 4] for g in range(4)]
        rows.append(
            jnp.where(
                group < 2,
                jnp.where(group == 0, pick[0], pick[1]),
                jnp.where(group == 2, pick[2], pick[3]),
            )
        )
    return jnp.concatenate(rows, axis=0)


def rows_form(high, low):
    return jnp.concatenate([high, high, low, low], axis=0)


def lanes_form(m):
    high = m.astype(BF16).astype(F32)
    v = jnp.where(lane_group(m.shape) < 2, high, m - high).astype(BF16)
    return jnp.concatenate([v] * 4, axis=0)


def kernel(
    dens,
    bases,
    blocks,
    nsrc,
    sleaf,
    fsrc,
    coup,
    loc_t,
    up_t,
    up_c,
    out,
    own,
    buf,
    stage,
    bas_v,
    blk_v,
    cpl_v,
    loc_v,
    upt_v,
    upc_v,
    ef,
    uf,
    cf,
    e_hi,
    e_lo,
    e_v,
    b_hi,
    b_lo,
    f_rep,
    x_up,
    x_dn,
    ll,
    acc,
    lvl,
    lrecv,
    part,
    rbuf,
    own_sem,
    loc_sem,
    xs_sem,
    xr_sem,
    hs_sem,
    hr_sem,
    ys_sem,
    yr_sem,
    ls_sem,
    lr_sem,
    rs_sem,
    rr_sem,
):
    d = lax.axis_index("leaf")
    me = lax.axis_index("rhs")
    my_rows = pl.ds(pl.multiple_of(me * COLS, COLS), COLS)

    def leaf_at(offset):
        return lax.rem(d + (offset + 2 * NLEAF), NLEAF)

    def rhs_at(offset):
        return lax.rem(me + offset, NRHS)

    barrier = pltpu.get_barrier_semaphore()
    for offset in (1, 2, 3):
        pl.semaphore_signal(barrier, inc=1, device_id={"rhs": rhs_at(offset)}, device_id_type=MESH)
    for offset in GREET:
        pl.semaphore_signal(
            barrier, inc=1, device_id={"leaf": leaf_at(offset)}, device_id_type=MESH
        )

    def own_copy(k):
        return pltpu.make_async_copy(
            dens.at[:, pl.ds(pl.multiple_of(k * WIDTH, WIDTH), WIDTH)], own.at[k], own_sem.at[k]
        )

    pairs = (
        (bases, bas_v),
        (loc_t, loc_v),
        (blocks, blk_v),
        (up_t, upt_v),
        (up_c, upc_v),
        (coup, cpl_v),
    )
    loads = [pltpu.make_async_copy(s, v, loc_sem.at[i]) for i, (s, v) in enumerate(pairs)]

    @pl.loop(0, LEAVES)
    def _(k):
        own_copy(k).start()

    for load in loads:
        load.start()

    @pl.loop(0, LEAVES)
    def _(k):
        own_copy(k).wait()

    for j in range(6):
        for c in range(4):
            wanted = jnp.maximum(sleaf[j, c, d], 0)
            stage[j, c] = own[wanted]

    @pl.loop(0, LEAVES, unroll=8)
    def _(k):
        buf[k, my_rows, :] = own[k]

    pl.semaphore_wait(barrier, 3 + len(GREET))

    own_sends = [
        pltpu.make_async_remote_copy(
            src_ref=own,
            dst_ref=buf.at[pl.ds(0, LEAVES), my_rows, :],
            send_sem=xs_sem.at[o - 1],
            recv_sem=xr_sem.at[o - 1],
            device_id={"rhs": rhs_at(o)},
            device_id_type=MESH,
        )
        for o in (1, 2, 3)
    ]
    halo_sends = [
        pltpu.make_async_remote_copy(
            src_ref=stage.at[j],
            dst_ref=buf.at[pl.ds(LEAVES + 4 * j, 4), my_rows, :],
            send_sem=hs_sem.at[j],
            recv_sem=hr_sem.at[j],
            device_id={"leaf": leaf_at(FACES[j])},
            device_id_type=MESH,
        )
        for j in range(6)
    ]
    for send in halo_sends:
        send.start()
    for send in own_sends:
        send.start()

    loads[0].wait()

    @pl.loop(0, LEAVES, unroll=4)
    def _(t):
        b = bas_v[:, pl.ds(pl.multiple_of(t * WIDTH, WIDTH), WIDTH)]
        high, low = halves(b)
        b_hi[t] = high
        b_lo[t] = low
        w = jnp.concatenate([high, low], axis=1)
        x = own[t]
        r = dot_nt(jnp.concatenate([x, x], axis=1), jnp.concatenate([w] * 4, axis=0))
        f_rep[t] = r
        x_up[LEAVES + t] = coef_form(r)

    loads[1].wait()
    for a in range(8):
        blk = jnp.concatenate([loc_v[8 * b + a] for b in range(4)], axis=0)
        ef[pl.ds(64 * a, 64), :] = blk.T

    @pl.loop(2, 64, unroll=2)
    def _(n):
        m = unfold(ef[pl.ds(n, 8, stride=64), :])
        high = m.astype(BF16)
        rest = m - high.astype(F32)
        e_hi[n] = high
        e_lo[n] = rest.astype(BF16)
        e_v[n] = jnp.where(lane_group(m.shape) < 2, high.astype(F32), rest).astype(BF16)

    def lift(p):
        x = jnp.concatenate([x_up[2 * p], x_up[2 * p + 1]], axis=1)
        w = jnp.concatenate(
            [
                rows_form(e_hi[2 * p], e_lo[2 * p]),
                rows_form(e_hi[2 * p + 1], e_lo[2 * p + 1]),
            ],
            axis=0,
        )
        x_up[p] = coef_form(dot_nn(x, w))

    for width in (16, 8, 4, 2, 1):

        @pl.loop(width, 2 * width, unroll=min(width, 4))
        def _(p):
            lift(p)

    lvl[0] = x_up[1]

    def level_sends(level):
        step = 2**level
        side = 1 - 2 * lax.rem(lax.div(d, step), 2)
        targets = [
            leaf_at(2 * step),
            leaf_at(-2 * step),
            lax.rem(d + 3 * step * side + 2 * NLEAF, NLEAF),
        ]
        if level < 4:
            targets.append(d + step * side)
        return [
            pltpu.make_async_remote_copy(
                src_ref=lvl.at[level],
                dst_ref=lrecv.at[level, i],
                send_sem=ls_sem.at[level, i],
                recv_sem=lr_sem.at[level, i],
                device_id={"leaf": target},
                device_id_type=MESH,
            )
            for i, target in enumerate(targets)
        ]

    sends = [level_sends(level) for level in range(5)]

    def start_level(level):
        for send in reversed(sends[level]):
            send.start()

    start_level(0)

    for send in halo_sends:
        send.wait_recv()
    halo_fwd = [
        pltpu.make_async_remote_copy(
            src_ref=buf.at[pl.ds(LEAVES, 24), my_rows, :],
            dst_ref=buf.at[pl.ds(LEAVES, 24), my_rows, :],
            send_sem=ys_sem.at[o - 1],
            recv_sem=yr_sem.at[o - 1],
            device_id={"rhs": rhs_at(o)},
            device_id_type=MESH,
        )
        for o in (1, 2, 3)
    ]
    for send in halo_fwd:
        send.start()

    loads[3].wait()
    for a in range(8):
        blk = jnp.concatenate([upt_v[8 * b + a] for b in range(4)], axis=0)
        uf[pl.ds(128 * a, 128), :] = blk.T
    loads[4].wait()
    for c in range(3):
        for a in range(8):
            blk = jnp.concatenate([upc_v[c, 8 * b + a] for b in range(4)], axis=0)
            cf[pl.ds(1024 * c + 128 * a, 128), :] = blk.T

    def node_at(level):
        return lax.div(d + NLEAF, 2**level)

    def lift_level(level):
        n = node_at(level)
        twin = n + 1 - 2 * lax.rem(n, 2)
        x = jnp.concatenate([lvl[level], lrecv[level, 3]], axis=1)
        w = jnp.concatenate(
            [
                rows_form(*halves(unfold(uf[pl.ds(n, 8, stride=128), :]))),
                rows_form(*halves(unfold(uf[pl.ds(twin, 8, stride=128), :]))),
            ],
            axis=0,
        )
        lvl[level + 1] = coef_form(dot_nn(x, w))

    def leaf_coupling(first, count):
        @pl.loop(first, first + count, unroll=2)
        def _(t):
            group = lane_group((COLS, 128))
            x_high, x_low, c_high, c_low = [], [], [], []
            for half in range(2):
                g = [f_rep[fsrc[4 * half + j, t]] for j in range(4)]
                g = jnp.where(
                    group < 2,
                    jnp.where(group == 0, g[0], g[1]),
                    jnp.where(group == 2, g[2], g[3]),
                )
                high, low = halves(g)
                x_high.append(high)
                x_low.append(low)
                m = jnp.concatenate([cpl_v[t, 4 * half + j] for j in range(4)], axis=1)
                high, low = halves(m)
                c_high.append(high)
                c_low.append(low)
            x = jnp.concatenate(x_high + x_low + x_high, axis=1)
            w = jnp.concatenate(c_high + c_high + c_low, axis=1)
            ll[t] = dot_nt(x, jnp.concatenate([w] * 4, axis=0))

    loads[5].wait()
    for level in range(4):
        leaf_coupling(8 * level, 8)
        sends[level][3].wait_recv()
        lift_level(level)
        start_level(level + 1)

    loads[2].wait()
    for send in own_sends + halo_fwd:
        send.wait_recv()
    part_sends = []
    for chunk in range(CHUNKS):

        @pl.loop(chunk * CHUNK, (chunk + 1) * CHUNK, unroll=4)
        def _(t):
            x = jnp.concatenate([buf[nsrc[0, t]], buf[nsrc[1, t]]], axis=1)
            w = jnp.concatenate([blk_v[t, 0], blk_v[t, 1]], axis=1)
            o = dot_nt(x, w)
            for q in range(NRHS):
                part[q, t] = o[COLS * q : COLS * (q + 1)]

        for o in (2, 1, 3):
            piece = pl.ds(chunk * CHUNK, CHUNK)
            send = pltpu.make_async_remote_copy(
                src_ref=part.at[rhs_at(o), piece],
                dst_ref=rbuf.at[o - 1, piece],
                send_sem=rs_sem.at[o - 1, chunk],
                recv_sem=rr_sem.at[o - 1, chunk],
                device_id={"rhs": rhs_at(o)},
                device_id_type=MESH,
            )
            send.start()
            part_sends.append(send)

    field = None
    for level in (4, 3, 2, 1, 0):
        width = NLEAF // 2**level
        n = node_at(level)
        t = n - width
        even = lax.rem(t, 2) == 0
        valid = [t + 2 <= width - 1, t >= 2, jnp.where(even, t + 3 <= width - 1, t >= 3)]
        for send in sends[level][:3]:
            send.wait_recv()
        xs, ws = [], []
        for slot, ok, c in ((0, valid[1], 0), (1, valid[0], 1), (2, valid[2], 2)):
            got = lrecv[level, slot].astype(F32)
            xs.append((got * ok.astype(F32)).astype(BF16))
            ws.append(lanes_form(unfold(cf[pl.ds(1024 * c + n, 8, stride=128), :])))
        if field is not None:
            xs.append(coef_form(field))
            ws.append(lanes_form(unfold(uf[pl.ds(n, 8, stride=128), :])))
        field = dot_nt(jnp.concatenate(xs, axis=1), jnp.concatenate(ws, axis=1))

    x_dn[1] = coef_form(field)
    for width in (2, 4, 8, 16):

        @pl.loop(width, 2 * width, unroll=min(width, 4))
        def _(h):
            r = dot_nt(x_dn[lax.div(h, 2)], jnp.concatenate([e_v[h]] * 4, axis=0))
            x_dn[h] = coef_form(r)

    @pl.loop(0, LEAVES, unroll=4)
    def _(t):
        h = t + LEAVES
        r = dot_nt(x_dn[lax.div(h, 2)], jnp.concatenate([e_v[h]] * 4, axis=0))
        x = coef_form(r + ll[t])
        acc[t] = dot_nn(x, rows_form(b_hi[t], b_lo[t]))

    for chunk in range(CHUNKS):
        for send in part_sends[3 * chunk : 3 * chunk + 3]:
            send.wait_recv()

        @pl.loop(chunk * CHUNK, (chunk + 1) * CHUNK, unroll=4)
        def _(t):
            near = (part[me, t] + rbuf[0, t]) + (rbuf[1, t] + rbuf[2, t])
            out[:, pl.ds(pl.multiple_of(t * WIDTH, WIDTH), WIDTH)] = near + acc[t]

    for send in own_sends + halo_sends + halo_fwd + part_sends:
        send.wait_send()
    for group in sends:
        for send in group:
            send.wait_send()


def local(dens, bases, blocks, near_src, send_leaf, far_src, coupling, local_t, upper_t, up_c):
    any_spec = pl.BlockSpec(memory_space=pl.ANY)
    smem_spec = pl.BlockSpec(memory_space=pltpu.SMEM)
    dma = pltpu.SemaphoreType.DMA
    vmem = pltpu.VMEM
    return pl.pallas_call(
        kernel,
        out_shape=jax.ShapeDtypeStruct((COLS, LEAVES * WIDTH), F32),
        in_specs=[any_spec] * 3 + [smem_spec] * 3 + [any_spec] * 4,
        out_specs=pl.BlockSpec(memory_space=pltpu.VMEM),
        scratch_shapes=[
            vmem((LEAVES, COLS, WIDTH), BF16),
            vmem((SLOTS, NRHS * COLS, WIDTH), BF16),
            vmem((6, 4, COLS, WIDTH), BF16),
            vmem((32, LEAVES * WIDTH), F32),
            vmem((LEAVES, 2, WIDTH, WIDTH), BF16),
            vmem((LEAVES, 8, 32, 32), F32),
            vmem((32, 32, 64), F32),
            vmem((32, 32, 128), F32),
            vmem((3, 32, 32, 128), F32),
            vmem((512, 128), F32),
            vmem((1024, 128), F32),
            vmem((3072, 128), F32),
            vmem((64, 32, 128), BF16),
            vmem((64, 32, 128), BF16),
            vmem((64, 32, 128), BF16),
            vmem((LEAVES, 32, 128), BF16),
            vmem((LEAVES, 32, 128), BF16),
            vmem((LEAVES, COLS, 128), F32),
            vmem((64, COLS, 128), BF16),
            vmem((LEAVES, COLS, 128), BF16),
            vmem((LEAVES, COLS, 128), F32),
            vmem((LEAVES, COLS, 128), F32),
            vmem((5, COLS, 128), BF16),
            vmem((5, 4, COLS, 128), BF16),
            vmem((NRHS, LEAVES, COLS, WIDTH), F32),
            vmem((3, LEAVES, COLS, WIDTH), F32),
            dma((LEAVES,)),
            dma((6,)),
            dma((3,)),
            dma((3,)),
            dma((6,)),
            dma((6,)),
            dma((3,)),
            dma((3,)),
            dma((5, 4)),
            dma((5, 4)),
            dma((3, CHUNKS)),
            dma((3, CHUNKS)),
        ],
        compiler_params=pltpu.CompilerParams(
            collective_id=0, has_side_effects=True, vmem_limit_bytes=48 * 2**20
        ),
        name="h2_product",
    )(
        dens,
        bases,
        blocks,
        near_src.T,
        send_leaf.transpose(1, 2, 0),
        far_src.T,
        coupling,
        local_t[0].transpose(1, 2, 0),
        upper_t.transpose(1, 2, 0),
        up_c.transpose(1, 2, 3, 0),
    )


def solution(mesh):
    in_specs = (
        P("rhs", "leaf"),
        P(None, "leaf"),
        P("leaf", "rhs", None, None),
        P("leaf", "rhs"),
        P(),
        P("leaf", None),
        P("leaf", None, None, None),
        P("leaf", None, None, None),
        P(),
        P(),
    )
    return jax.shard_map(
        local, mesh=mesh, in_specs=in_specs, out_specs=P("rhs", "leaf"), check_vma=False
    )
```

time: 179 us -> 55.2 us (0.31)
  local copies, waits for them, and re-layouts: 70.7 us -> 9.8 us
  Pallas kernels: 0 us -> 44.8 us
  matrix products: 32.5 us -> 0 us
  starting transfers between devices: 31.4 us -> 0 us
  other arithmetic: 17.6 us -> 0 us
  between operations: 14.3 us -> 0.02 us
  blocking collectives: 10.2 us -> 0 us
    pallas_call x0 -> x1, Pallas kernels: none -> 44.8 us  [local(): pl.pallas_call(kernel, out_shape=jax.ShapeDtypeStruct((COLS, LEAVES * WID...]
    dot_general x37 -> x0, matrix products: 32.5 us -> none  [the longest x24 17.2 us: apply_maps(): jnp.einsum('...nrs,...nqs->...nqr', node_maps, coef_rows, precision=TOP_P...]
    unnamed x113 -> x19, local copies, waits for them, and re-layouts: 40 us -> 9.8 us
    ppermute x6 -> x0, starting transfers between devices: 23 us -> none  [shifted(): lax.ppermute(value, axis, [(source, source + steps) for source in range(f...]
    slice x14 -> x0, local copies, waits for them, and re-layouts: 13.1 us -> none  [the longest x3 4.83 us: couple_level(): maps_level[:, 1]]
    gather x8 -> x0, local copies, waits for them, and re-layouts: 12.8 us -> none  [the longest x6 8.61 us: local(): chosen = jnp.take(neighbour_panels, jnp.maximum(sent_leaf, 0), axis=1)]
    all_gather x1 -> x0, blocking collectives: 10.2 us -> none  [local(): piece_sources = lax.all_gather(near_src, 'rhs', axis=1, tiled=True)]
    all_to_all x1 -> x0, starting transfers between devices: 8.39 us -> none  [from_everyone(): return lax.all_to_all(copies, axis, split_axis=0, concat_axis=0, tiled=True)]
  transfers between devices with their start and end apart: 8 -> 0, of which waited for: 0 -> 0; matrix products, arithmetic and copies ran while one was open for 63% -> 0% of each run, Pallas kernels for 0% -> 0%
where the time goes in v1:
time: 55.2 us; the launch traced here: 54.6 us
  Pallas kernels  44.8 us (81%)
  local copies, waits for them, and re-layouts  9.8 us (18%)
    pallas_call x1, Pallas kernels, local(): pl.pallas_call(kernel, out_shape=jax.ShapeDtypeStruct((COLS, LEAVES * WID...  44.8 us
    unnamed x19, local copies, waits for them, and re-layouts  9.8 us

profile of v1, /device:TPU:32, one launch (start us, length us, event | category | flops | bytes accessed | tf_op | source)
XLA Modules:
  0.0 54.6 jit_solution(2514933259024256829)
XLA Ops:
  0.0 0.0 copy-start
  0.0 1.6 %copy-done = bf16[32,2,128,128]{3,2,1,0:T(8,128)(2,1)S(1)} copy-done((bf16[32,2,128,128]{3,2,1,0:T(8,128)(2,1)S(1)}, bf16[32,2,128,128]{3,2,1,0:T(8,128)(2,1)}, u32[]{:S(2)}) %copy-start) | copy-done | bytes 2097176
  1.6 0.0 copy-start.1
  1.6 1.4 %copy-done.1 = f32[128,3,32,32]{0,3,2,1:T(8,128)S(1)} copy-done((f32[128,3,32,32]{0,3,2,1:T(8,128)S(1)}, f32[128,3,32,32]{0,3,2,1:T(8,128)}, u32[]{:S(2)}) %copy-start.1) | copy-done | bytes 1572888
  3.0 0.0 copy-start.2
  3.0 1.0 %copy-done.2 = f32[32,4096]{1,0:T(8,128)S(1)} copy-done((f32[32,4096]{1,0:T(8,128)S(1)}, f32[32,4096]{1,0:T(8,128)}, u32[]{:S(2)}) %copy-start.2) | copy-done | bytes 524312
  4.0 0.0 copy-start.3
  4.0 1.0 %copy-done.3 = f32[1,64,32,32]{1,3,2,0:T(8,128)S(1)} copy-done((f32[1,64,32,32]{1,3,2,0:T(8,128)S(1)}, f32[1,64,32,32]{1,3,2,0:T(8,128)}, u32[]{:S(2)}) %copy-start.3) | copy-done | bytes 262168
  5.1 0.0 copy-start.4
  5.1 1.0 %copy-done.4 = f32[128,32,32]{0,2,1:T(8,128)S(1)} copy-done((f32[128,32,32]{0,2,1:T(8,128)S(1)}, f32[128,32,32]{0,2,1:T(8,128)}, u32[]{:S(2)}) %copy-start.4) | copy-done | bytes 524312
  6.1 0.0 copy-start.5
  6.1 0.9 %copy-done.5 = bf16[16,4096]{1,0:T(8,128)(2,1)S(1)} copy-done((bf16[16,4096]{1,0:T(8,128)(2,1)S(1)}, bf16[16,4096]{1,0:T(8,128)(2,1)}, u32[]{:S(2)}) %copy-start.5) | copy-done | bytes 131096
  7.0 0.0 copy-start.6
  7.0 0.7 %copy-done.6 = s32[64,6,4]{0,2,1:T(4,128)S(1)} copy-done((s32[64,6,4]{0,2,1:T(4,128)S(1)}, s32[64,6,4]{0,2,1:T(4,128)}, u32[]{:S(2)}) %copy-start.6) | copy-done | bytes 6168
  7.7 0.0 copy-start.7
  7.7 0.7 %copy-done.7 = s32[32,8]{0,1:T(8,128)S(1)} copy-done((s32[32,8]{0,1:T(8,128)S(1)}, s32[32,8]{0,1:T(8,128)}, u32[]{:S(2)}) %copy-start.7) | copy-done | bytes 1048
  8.4 0.0 copy-start.8
  8.4 0.7 %copy-done.8 = s32[32,2]{0,1:T(2,128)S(1)} copy-done((s32[32,2]{0,1:T(2,128)S(1)}, s32[32,2]{0,1:T(2,128)}, u32[]{:S(2)}) %copy-start.8) | copy-done | bytes 280
  9.1 44.8 %h2_product.1 = f32[16,4096]{1,0:T(8,128)S(1)} custom-call(bf16[16,4096]{1,0:T(8,128)(2,1)S(1)} %copy-done.5, f32[32,4096]{1,0:T(8,128)S(1)} %copy-done.2, bf16[32,2,128,128]{3,2,1,0:T(8,128)(2,1)S(1)} %copy-done, s32[2,32]{1,0:T(2,128)S(1)} %bitcast.13, s32[6,4,64]{2,1,0:T(4,128)S(1)} %bitcast.11, s32[8,32]{1,0:T(8,128)S(1)} %bitcast.12, ...), custom_call_target="tpu_custom_call" | custom-call | tf_op jit(solution)/shard_map/h2_product/pallas_call | solution.py:438
  53.9 0.7 %copy.12 = f32[16,4096]{1,0:T(8,128)} copy(f32[16,4096]{1,0:T(8,128)S(1)} %h2_product.1) | data formatting | bytes 524288
Async XLA Ops:
  0.0 1.6 %copy-start = (bf16[32,2,128,128]{3,2,1,0:T(8,128)(2,1)S(1)}, bf16[32,2,128,128]{3,2,1,0:T(8,128)(2,1)}, u32[]{:S(2)}) copy-start(bf16[32,2,128,128]{3,2,1,0:T(8,128)(2,1)} %blocks.1) | copy-start | bytes 6291460
  1.6 1.4 %copy-start.1 = (f32[128,3,32,32]{0,3,2,1:T(8,128)S(1)}, f32[128,3,32,32]{0,3,2,1:T(8,128)}, u32[]{:S(2)}) copy-start(f32[128,3,32,32]{0,3,2,1:T(8,128)} %param.19) | copy-start | bytes 4718596
  3.0 1.0 %copy-start.2 = (f32[32,4096]{1,0:T(8,128)S(1)}, f32[32,4096]{1,0:T(8,128)}, u32[]{:S(2)}) copy-start(f32[32,4096]{1,0:T(8,128)} %bases.1) | copy-start | bytes 1572868
  4.0 1.0 %copy-start.3 = (f32[1,64,32,32]{1,3,2,0:T(8,128)S(1)}, f32[1,64,32,32]{1,3,2,0:T(8,128)}, u32[]{:S(2)}) copy-start(f32[1,64,32,32]{1,3,2,0:T(8,128)} %param.17) | copy-start | bytes 786436
  5.1 1.0 %copy-start.4 = (f32[128,32,32]{0,2,1:T(8,128)S(1)}, f32[128,32,32]{0,2,1:T(8,128)}, u32[]{:S(2)}) copy-start(f32[128,32,32]{0,2,1:T(8,128)} %param.18) | copy-start | bytes 1572868
  6.1 0.9 %copy-start.5 = (bf16[16,4096]{1,0:T(8,128)(2,1)S(1)}, bf16[16,4096]{1,0:T(8,128)(2,1)}, u32[]{:S(2)}) copy-start(bf16[16,4096]{1,0:T(8,128)(2,1)} %dens.1) | copy-start | bytes 393220
  7.0 0.7 %copy-start.6 = (s32[64,6,4]{0,2,1:T(4,128)S(1)}, s32[64,6,4]{0,2,1:T(4,128)}, u32[]{:S(2)}) copy-start(s32[64,6,4]{0,2,1:T(4,128)} %param.14) | copy-start | bytes 18436
  7.7 0.7 %copy-start.7 = (s32[32,8]{0,1:T(8,128)S(1)}, s32[32,8]{0,1:T(8,128)}, u32[]{:S(2)}) copy-start(s32[32,8]{0,1:T(8,128)} %param.15) | copy-start | bytes 3076
  8.4 0.7 %copy-start.8 = (s32[32,2]{0,1:T(2,128)S(1)}, s32[32,2]{0,1:T(2,128)}, u32[]{:S(2)}) copy-start(s32[32,2]{0,1:T(2,128)} %param.13) | copy-start | bytes 772

commit v2 on v1

--- a/solution.py
+++ b/solution.py
@@ -75,14 +75,17 @@
     dens,
     bases,
     blocks,
-    nsrc,
-    sleaf,
-    fsrc,
+    nsrc_h,
+    sleaf_h,
+    fsrc_h,
     coup,
     loc_t,
     up_t,
     up_c,
     out,
+    nsrc,
+    sleaf,
+    fsrc,
     own,
     buf,
     stage,
@@ -152,6 +155,9 @@
         (up_t, upt_v),
         (up_c, upc_v),
         (coup, cpl_v),
+        (nsrc_h, nsrc),
+        (sleaf_h, sleaf),
+        (fsrc_h, fsrc),
     )
     loads = [pltpu.make_async_copy(s, v, loc_sem.at[i]) for i, (s, v) in enumerate(pairs)]
 
@@ -159,12 +165,15 @@
     def _(k):
         own_copy(k).start()
 
-    for load in loads:
+    loads[7].start()
+    for load in loads[:7] + loads[8:]:
         load.start()
 
     @pl.loop(0, LEAVES)
     def _(k):
         own_copy(k).wait()
+
+    loads[7].wait()
 
     for j in range(6):
         for c in range(4):
@@ -347,6 +356,7 @@
             ll[t] = dot_nt(x, jnp.concatenate([w] * 4, axis=0))
 
     loads[5].wait()
+    loads[8].wait()
     for level in range(4):
         leaf_coupling(8 * level, 8)
         sends[level][3].wait_recv()
@@ -354,6 +364,7 @@
         start_level(level + 1)
 
     loads[2].wait()
+    loads[6].wait()
     for send in own_sends + halo_fwd:
         send.wait_recv()
     part_sends = []
@@ -431,16 +442,18 @@
 
 
 def local(dens, bases, blocks, near_src, send_leaf, far_src, coupling, local_t, upper_t, up_c):
-    any_spec = pl.BlockSpec(memory_space=pl.ANY)
-    smem_spec = pl.BlockSpec(memory_space=pltpu.SMEM)
+    any_spec = pl.BlockSpec(memory_space=pltpu.HBM)
     dma = pltpu.SemaphoreType.DMA
     vmem = pltpu.VMEM
     return pl.pallas_call(
         kernel,
         out_shape=jax.ShapeDtypeStruct((COLS, LEAVES * WIDTH), F32),
-        in_specs=[any_spec] * 3 + [smem_spec] * 3 + [any_spec] * 4,
+        in_specs=[any_spec] * 10,
         out_specs=pl.BlockSpec(memory_space=pltpu.VMEM),
         scratch_shapes=[
+            pltpu.SMEM((2, LEAVES), jnp.int32),
+            pltpu.SMEM((6, 4, NLEAF), jnp.int32),
+            pltpu.SMEM((8, LEAVES), jnp.int32),
             vmem((LEAVES, COLS, WIDTH), BF16),
             vmem((SLOTS, NRHS * COLS, WIDTH), BF16),
             vmem((6, 4, COLS, WIDTH), BF16),
@@ -468,7 +481,7 @@
             vmem((NRHS, LEAVES, COLS, WIDTH), F32),
             vmem((3, LEAVES, COLS, WIDTH), F32),
             dma((LEAVES,)),
-            dma((6,)),
+            dma((9,)),
             dma((3,)),
             dma((3,)),
             dma((6,)),
@@ -481,7 +494,7 @@
             dma((3, CHUNKS)),
         ],
         compiler_params=pltpu.CompilerParams(
-            collective_id=0, has_side_effects=True, vmem_limit_bytes=48 * 2**20
+            collective_id=0, has_side_effects=True, vmem_limit_bytes=60 * 2**20
         ),
         name="h2_product",
     )(

time: 55.2 us -> 46.6 us (0.84)
  local copies, waits for them, and re-layouts: 9.8 us -> 1.67 us
    unnamed x19 -> x1, local copies, waits for them, and re-layouts: 9.8 us -> 1.67 us
where the time goes in v2:
time: 46.6 us; the launch traced here: 46.4 us
  Pallas kernels  44.7 us (96%)
  local copies, waits for them, and re-layouts  1.67 us (4%)
    pallas_call x1, Pallas kernels, local(): pl.pallas_call(kernel, out_shape=jax.ShapeDtypeStruct((COLS, LEAVES * WID...  44.7 us
    unnamed x1, local copies, waits for them, and re-layouts  1.67 us

profile of v2, /device:TPU:32, one launch (start us, length us, event | category | flops | bytes accessed | tf_op | source)
XLA Modules:
  0.0 46.4 jit_solution(3343166194073425525)
XLA Ops:
  0.0 44.7 %h2_product.1 = f32[16,4096]{1,0:T(8,128)} custom-call(bf16[16,4096]{1,0:T(8,128)(2,1)} %dens.1, f32[32,4096]{1,0:T(8,128)} %bases.1, bf16[32,2,128,128]{3,2,1,0:T(8,128)(2,1)} %blocks.1, s32[2,32]{1,0:T(2,128)} %bitcast.13, s32[6,4,64]{2,1,0:T(4,128)} %bitcast.11, s32[8,32]{1,0:T(8,128)} %bitcast.12, f32[32,8,32,32]{3,2,1,0:T(8,128)} %coup.1, ...), custom_call_target="tpu_custom_call" | custom-call | tf_op jit(solution)/shard_map/h2_product/pallas_call | solution.py:448
  44.7 1.7 %copy.12 = f32[16,4096]{1,0:T(8,128)} copy(f32[16,4096]{1,0:T(8,128)} %h2_product.1) | data formatting | bytes 524288

commit v3 on v2

v3 whole, which is shorter than its diff:
```python
import functools

import jax
import jax.numpy as jnp
from jax import lax
from jax.experimental import pallas as pl
from jax.experimental.pallas import tpu as pltpu
from jax.sharding import PartitionSpec as P

F32 = jnp.float32
BF16 = jnp.bfloat16
MESH = pl.DeviceIdType.MESH
LEAVES = 32
WIDTH = 128
COLS = 16
NLEAF = 64
NRHS = 4
SLOTS = 56
FACES = (1, -1, 4, -4, 16, -16)
GREET = (1, -1, 3, -3) + tuple(range(2, 64, 2))


def dot_nn(a, b):
    return lax.dot_general(a, b, (((1,), (0,)), ((), ())), preferred_element_type=F32)


def dot_nt(a, b):
    return lax.dot_general(a, b, (((1,), (1,)), ((), ())), preferred_element_type=F32)


def halves(x):
    high = x.astype(BF16)
    return high, (x - high.astype(F32)).astype(BF16)


def lane_group(shape):
    return lax.broadcasted_iota(jnp.int32, shape, len(shape) - 1) // 32


def coef_form(r):
    group = lane_group(r.shape)
    high = r.astype(BF16).astype(F32)
    return jnp.where(group % 2 == 0, high, r - high).astype(BF16)


def unfold(tile):
    group = lane_group(tile.shape)
    turned = [tile] + [pltpu.roll(tile, 32 * k, 1) for k in (1, 2, 3)]
    rows = []
    for b in range(4):
        pick = [turned[(g - b) % 4] for g in range(4)]
        rows.append(
            jnp.where(
                group < 2,
                jnp.where(group == 0, pick[0], pick[1]),
                jnp.where(group == 2, pick[2], pick[3]),
            )
        )
    return jnp.concatenate(rows, axis=0)


def rows_form(high, low):
    return jnp.concatenate([high, high, low, low], axis=0)


def lanes_form(m):
    high = m.astype(BF16).astype(F32)
    v = jnp.where(lane_group(m.shape) < 2, high, m - high).astype(BF16)
    return jnp.concatenate([v] * 4, axis=0)


def kernel(
    dens,
    bases,
    blocks,
    nsrc_h,
    sleaf_h,
    fsrc_h,
    coup,
    loc_t,
    up_t,
    up_c,
    out,
    nsrc,
    sleaf,
    fsrc,
    own,
    buf,
    stage,
    bas_v,
    blk_v,
    cpl_v,
    loc_v,
    upt_v,
    upc_v,
    ef,
    uf,
    cf,
    e_v,
    b_hi,
    b_lo,
    q_hi,
    q_lo,
    t_x,
    f_rep,
    acc,
    m_rep,
    m_hi,
    m_lo,
    root_x,
    pair_x,
    lrecv,
    chips,
    part,
    raw,
    rbuf,
    own_sem,
    loc_sem,
    os_sem,
    or_sem,
    hs_sem,
    hr_sem,
    ys_sem,
    yr_sem,
    ls_sem,
    lr_sem,
    gs_sem,
    gr_sem,
    ps_sem,
    pr_sem,
):
    d = lax.axis_index("leaf")
    me = lax.axis_index("rhs")

    def leaf_at(offset):
        return lax.rem(d + (offset + 2 * NLEAF), NLEAF)

    def rhs_at(offset):
        return lax.rem(me + offset, NRHS)

    right, across, left = rhs_at(1), rhs_at(2), rhs_at(3)

    def rows_of(r):
        return pl.ds(pl.multiple_of(r * COLS, COLS), COLS)

    my_rows = rows_of(me)

    barrier = pltpu.get_barrier_semaphore()
    for peer in (right, left):
        pl.semaphore_signal(barrier, inc=1, device_id={"rhs": peer}, device_id_type=MESH)
    for offset in GREET:
        pl.semaphore_signal(
            barrier, inc=1, device_id={"leaf": leaf_at(offset)}, device_id_type=MESH
        )

    def own_copy(k):
        return pltpu.make_async_copy(
            dens.at[:, pl.ds(pl.multiple_of(k * WIDTH, WIDTH), WIDTH)], own.at[k], own_sem.at[k]
        )

    pairs = (
        (loc_t, loc_v),
        (bases, bas_v),
        (sleaf_h, sleaf),
        (up_t, upt_v),
        (coup, cpl_v),
        (fsrc_h, fsrc),
        (blocks, blk_v),
        (nsrc_h, nsrc),
        (up_c, upc_v),
    )
    loads = [pltpu.make_async_copy(s, v, loc_sem.at[i]) for i, (s, v) in enumerate(pairs)]
    for load in loads[:3]:
        load.start()

    @pl.loop(0, LEAVES)
    def _(k):
        own_copy(k).start()

    for load in loads[3:]:
        load.start()

    loads[0].wait()
    for a in range(8):
        blk = jnp.concatenate([loc_v[pl.ds(32 * (8 * b + a), 32), :] for b in range(4)], axis=0)
        ef[pl.ds(64 * a, 64), :] = blk.T

    @pl.loop(0, 64, unroll=8)
    def _(n):
        m = unfold(ef[pl.ds(n, 8, stride=64), :])
        high = m.astype(BF16).astype(F32)
        e_v[n] = jnp.where(lane_group(m.shape) < 2, high, m - high).astype(BF16)

    row = lax.broadcasted_iota(jnp.int32, (32, 128), 0)
    lane = lax.broadcasted_iota(jnp.int32, (32, 128), 1)
    t_x[1] = jnp.where((lane % 64) == row, 1.0, 0.0).astype(BF16)
    for width in (2, 4, 8, 16, 32):
        for p in range(width // 2, width):
            w = jnp.concatenate([e_v[2 * p], e_v[2 * p + 1]], axis=0)
            r = dot_nt(t_x[p], w)
            t_x[2 * p] = coef_form(jnp.concatenate([r[:, :32]] * 4, axis=1))
            t_x[2 * p + 1] = coef_form(jnp.concatenate([r[:, 32:]] * 4, axis=1))

    loads[1].wait()

    @pl.loop(0, LEAVES, unroll=8)
    def _(t):
        high, low = halves(bas_v[:, pl.ds(pl.multiple_of(t * WIDTH, WIDTH), WIDTH)])
        b_hi[t] = high
        b_lo[t] = low
        high, low = halves(dot_nn(t_x[LEAVES + t], rows_form(high, low)))
        q_hi[t] = high
        q_lo[t] = low

    @pl.loop(0, LEAVES)
    def _(k):
        own_copy(k).wait()

    root = jnp.zeros((COLS, 32), F32)
    for t in range(LEAVES):
        x = own[t]
        root = root + dot_nt(
            jnp.concatenate([x, x], axis=1), jnp.concatenate([q_hi[t], q_lo[t]], axis=1)
        )
    root_x[...] = coef_form(jnp.concatenate([root] * 4, axis=1))

    loads[2].wait()
    for j in range(6):
        for c in range(4):
            wanted = jnp.maximum(sleaf[j, c, d], 0)
            stage[j, c] = own[wanted]

    @pl.loop(0, LEAVES, unroll=8)
    def _(k):
        buf[k, my_rows, :] = own[k]

    pl.semaphore_wait(barrier, 2 + len(GREET))

    side = 1 - 2 * lax.rem(d, 2)
    partners = (leaf_at(2), leaf_at(-2), lax.rem(d + 3 * side + NLEAF, NLEAF), d + side)
    root_sends = [
        pltpu.make_async_remote_copy(
            src_ref=root_x,
            dst_ref=lrecv.at[i],
            send_sem=ls_sem.at[i],
            recv_sem=lr_sem.at[i],
            device_id={"leaf": partner},
            device_id_type=MESH,
        )
        for i, partner in enumerate(partners)
    ]
    halo_sends = [
        pltpu.make_async_remote_copy(
            src_ref=stage.at[j],
            dst_ref=buf.at[pl.ds(LEAVES + 4 * j, 4), my_rows, :],
            send_sem=hs_sem.at[j],
            recv_sem=hr_sem.at[j],
            device_id={"leaf": leaf_at(FACES[j])},
            device_id_type=MESH,
        )
        for j in range(6)
    ]

    def over_rhs(src, dst, target, ssem, rsem):
        return pltpu.make_async_remote_copy(
            src_ref=src,
            dst_ref=dst,
            send_sem=ssem,
            recv_sem=rsem,
            device_id={"rhs": target},
            device_id_type=MESH,
        )

    def pass_on(slots, target, source, index, ssem, rsem):
        piece = buf.at[slots, rows_of(source), :]
        return over_rhs(piece, piece, target, ssem.at[index], rsem.at[index])

    lower, upper = pl.ds(0, 16), pl.ds(16, 16)
    own_out = [
        over_rhs(own.at[lower], buf.at[lower, my_rows, :], right, os_sem.at[0], or_sem.at[0]),
        over_rhs(own.at[upper], buf.at[upper, my_rows, :], left, os_sem.at[1], or_sem.at[1]),
        over_rhs(own.at[upper], buf.at[upper, my_rows, :], right, os_sem.at[2], or_sem.at[2]),
        over_rhs(own.at[lower], buf.at[lower, my_rows, :], left, os_sem.at[3], or_sem.at[3]),
    ]
    own_relay = [
        pass_on(lower, right, left, 4, os_sem, or_sem),
        pass_on(upper, left, right, 5, os_sem, or_sem),
    ]
    first, second = pl.ds(LEAVES, 12), pl.ds(LEAVES + 12, 12)
    halo_out = [
        pass_on(first, right, me, 0, ys_sem, yr_sem),
        pass_on(second, left, me, 1, ys_sem, yr_sem),
        pass_on(second, right, me, 2, ys_sem, yr_sem),
        pass_on(first, left, me, 3, ys_sem, yr_sem),
    ]
    halo_relay = [
        pass_on(first, right, left, 4, ys_sem, yr_sem),
        pass_on(second, left, right, 5, ys_sem, yr_sem),
    ]
    root_sends[3].start()
    for send in own_out + halo_sends + root_sends[:3]:
        send.start()

    @pl.loop(0, LEAVES, unroll=8)
    def _(t):
        w = jnp.concatenate([b_hi[t], b_lo[t]], axis=1)
        x = own[t]
        r = dot_nt(jnp.concatenate([x, x], axis=1), w)
        f_rep[t] = jnp.concatenate([r] * 4, axis=1)

    loads[3].wait()
    for a in range(8):
        blk = jnp.concatenate([upt_v[pl.ds(32 * (8 * b + a), 32), :] for b in range(4)], axis=0)
        uf[pl.ds(128 * a, 128), :] = blk.T

    def above(n):
        return unfold(uf[pl.ds(n, 8, stride=128), :])

    n0 = d + NLEAF
    chip = lax.div(d, 2)

    def leaf_coupling(begin, count):
        @pl.loop(begin, begin + count, unroll=4)
        def _(t):
            group = lane_group((COLS, 128))
            x_high, x_low, c_high, c_low = [], [], [], []
            for half in range(2):
                g = [f_rep[fsrc[4 * half + j, t]] for j in range(4)]
                g = jnp.where(
                    group < 2,
                    jnp.where(group == 0, g[0], g[1]),
                    jnp.where(group == 2, g[2], g[3]),
                )
                high, low = halves(g)
                x_high.append(high)
                x_low.append(low)
                m = jnp.concatenate([cpl_v[t, 4 * half + j] for j in range(4)], axis=1)
                high, low = halves(m)
                c_high.append(high)
                c_low.append(low)
            x = jnp.concatenate(x_high + x_low + x_high, axis=1)
            w = jnp.concatenate(c_high + c_high + c_low, axis=1)
            r = dot_nt(x, w)
            x = coef_form(jnp.concatenate([r] * 4, axis=1))
            acc[t] = dot_nn(x, rows_form(b_hi[t], b_lo[t]))

    root_sends[3].wait_recv()
    x = jnp.concatenate([root_x[...], lrecv[3]], axis=1)
    w = jnp.concatenate(
        [rows_form(*halves(above(n0))), rows_form(*halves(above(n0 + side)))], axis=0
    )
    pair = coef_form(dot_nn(x, w))
    pair_x[...] = pair
    chips[chip] = pair
    chip_sends = [
        pltpu.make_async_remote_copy(
            src_ref=pair_x,
            dst_ref=chips.at[chip],
            send_sem=gs_sem.at[k - 1],
            recv_sem=gr_sem.at[k - 1],
            device_id={"leaf": leaf_at(2 * k)},
            device_id_type=MESH,
        )
        for k in range(1, 32)
    ]
    for send in chip_sends:
        send.start()

    loads[4].wait()
    loads[5].wait()
    leaf_coupling(0, 8)

    for send in own_out[:2]:
        send.wait_recv()
    for send in own_relay:
        send.start()
    for send in halo_sends:
        send.wait_recv()
    for send in halo_out:
        send.start()

    leaf_coupling(8, 16)

    for send in halo_out[:2]:
        send.wait_recv()
    for send in halo_relay:
        send.start()

    leaf_coupling(24, 8)

    loads[6].wait()
    loads[7].wait()
    for send in own_out[2:] + own_relay + halo_out[2:] + halo_relay:
        send.wait_recv()

    def near(begin, count):
        @pl.loop(begin, begin + count, unroll=8)
        def _(t):
            x = jnp.concatenate([buf[nsrc[0, t]], buf[nsrc[1, t]]], axis=1)
            w = jnp.concatenate([blk_v[t, 0], blk_v[t, 1]], axis=1)
            o = dot_nt(x, w)
            for q in range(NRHS):
                part[q, t] = o[COLS * q : COLS * (q + 1)]

    def partial(index, dest, t0, count, target, landing):
        return over_rhs(
            part.at[dest, pl.ds(t0, count)], landing, target, ps_sem.at[index], pr_sem.at[index]
        )

    raw_sends = [
        partial(0, across, 0, 8, right, raw.at[0, pl.ds(0, 8)]),
        partial(1, across, 16, 8, left, raw.at[1, pl.ds(0, 8)]),
        partial(2, across, 8, 8, right, raw.at[0, pl.ds(8, 8)]),
        partial(3, across, 24, 8, left, raw.at[1, pl.ds(8, 8)]),
    ]
    plain_sends = [
        partial(4, right, 16, 16, right, rbuf.at[0, upper]),
        partial(5, left, 0, 16, left, rbuf.at[1, lower]),
    ]
    sum_sends = [
        partial(6, right, 0, 8, right, rbuf.at[0, pl.ds(0, 8)]),
        partial(7, left, 16, 8, left, rbuf.at[1, pl.ds(16, 8)]),
        partial(8, right, 8, 8, right, rbuf.at[0, pl.ds(8, 8)]),
        partial(9, left, 24, 8, left, rbuf.at[1, pl.ds(24, 8)]),
    ]
    for i, begin in enumerate((0, 16, 8, 24)):
        near(begin, 8)
        raw_sends[i].start()
    for send in plain_sends:
        send.start()

    def join(i):
        side_of, begin = ((0, 0), (1, 16), (0, 8), (1, 24))[i]
        dest = left if side_of else right
        raw_sends[i].wait_recv()

        @pl.loop(0, 8, unroll=8)
        def _(k):
            t = begin + k
            part[dest, t] = part[dest, t] + raw[side_of, t - 16 * side_of]

        sum_sends[i].start()

    loads[8].wait()
    for c in range(3):
        for a in range(8):
            blk = jnp.concatenate(
                [upc_v[c, pl.ds(8 * b + a, 32, stride=32), :] for b in range(4)], axis=0
            )
            cf[pl.ds(1024 * c + 128 * a, 128), :] = blk.T

    join(0)
    join(1)

    down = None
    couplings = {}
    for level in range(5):
        n = lax.div(n0, 2**level)
        width = NLEAF // 2**level
        t = n - width
        even = lax.rem(t, 2) == 0
        valid = (t >= 2, t + 2 < width, jnp.where(even, t + 3 < width, t >= 3))
        where_to = (n - 2, n + 2, n + 3 - 6 * lax.rem(t, 2))
        cts = []
        for c in range(3):
            ct = unfold(cf[pl.ds(1024 * c + n, 8, stride=128), :])
            cts.append(ct * valid[c].astype(F32))
        if level:
            left_side = jnp.concatenate([coef_form(ct) for ct in cts], axis=0)
            r = dot_nt(left_side, lanes_form(down))
            cts = [r[32 * c : 32 * (c + 1)] for c in range(3)]
        couplings[level] = [
            (jnp.where(ok, place, n), ct) for ok, place, ct in zip(valid, where_to, cts)
        ]
        if level == 0:
            down = above(n0)
        elif level < 4:
            down = dot_nn(coef_form(down), rows_form(*halves(above(n))))

    join(2)
    join(3)

    for n in range(4, 8):
        m_rep[n] = jnp.zeros((32, 128), F32)
    for level in (4, 3, 2, 1):
        width = NLEAF // 2**level
        if level < 4:
            for p in range(width // 2, width):
                lhs = jnp.concatenate(
                    [coef_form(above(2 * p)), coef_form(above(2 * p + 1))], axis=0
                )
                r = dot_nn(lhs, rows_form(*halves(m_rep[p])))
                m_rep[2 * p] = r[:32]
                m_rep[2 * p + 1] = r[32:]
        for place, ct in couplings[level]:
            m_rep[place] = m_rep[place] + ct

    @pl.loop(0, 32, unroll=4)
    def _(e):
        high, low = halves(m_rep[32 + e])
        m_hi[e] = high
        m_lo[e] = low

    for send in root_sends[:3]:
        send.wait_recv()
    field = jnp.zeros((COLS, 128), F32)
    for c in range(3):
        field = field + dot_nn(lrecv[c], rows_form(*halves(couplings[0][c][1])))
    for send in chip_sends:
        send.wait_recv()
    for e in range(0, 32, 2):
        x = jnp.concatenate([chips[e], chips[e + 1]], axis=1)
        w = jnp.concatenate(
            [rows_form(m_hi[e], m_lo[e]), rows_form(m_hi[e + 1], m_lo[e + 1])], axis=0
        )
        field = field + dot_nn(x, w)
    field_x = coef_form(field)

    def finish(begin, count):
        @pl.loop(begin, begin + count, unroll=8)
        def _(t):
            far = acc[t] + dot_nn(field_x, rows_form(q_hi[t], q_lo[t]))
            near_sum = part[me, t] + (rbuf[0, t] + rbuf[1, t])
            out[:, pl.ds(pl.multiple_of(t * WIDTH, WIDTH), WIDTH)] = near_sum + far

    for send in plain_sends + sum_sends:
        send.wait_recv()
    finish(0, LEAVES)

    for send in root_sends + halo_sends + own_out + own_relay + halo_out + halo_relay:
        send.wait_send()
    for send in chip_sends + raw_sends + plain_sends + sum_sends:
        send.wait_send()


def local(dens, bases, blocks, near_src, send_leaf, far_src, coupling, local_t, upper_t, up_c):
    any_spec = pl.BlockSpec(memory_space=pltpu.HBM)
    dma = pltpu.SemaphoreType.DMA
    vmem = pltpu.VMEM
    return pl.pallas_call(
        kernel,
        out_shape=jax.ShapeDtypeStruct((COLS, LEAVES * WIDTH), F32),
        in_specs=[any_spec] * 10,
        out_specs=pl.BlockSpec(memory_space=pltpu.VMEM),
        scratch_shapes=[
            pltpu.SMEM((2, LEAVES), jnp.int32),
            pltpu.SMEM((6, 4, NLEAF), jnp.int32),
            pltpu.SMEM((8, LEAVES), jnp.int32),
            vmem((LEAVES, COLS, WIDTH), BF16),
            vmem((SLOTS, NRHS * COLS, WIDTH), BF16),
            vmem((6, 4, COLS, WIDTH), BF16),
            vmem((32, LEAVES * WIDTH), F32),
            vmem((LEAVES, 2, WIDTH, WIDTH), BF16),
            vmem((LEAVES, 8, 32, 32), F32),
            vmem((1024, 64), F32),
            vmem((1024, 128), F32),
            vmem((3, 1024, 128), F32),
            vmem((512, 128), F32),
            vmem((1024, 128), F32),
            vmem((3072, 128), F32),
            vmem((64, 32, 128), BF16),
            vmem((LEAVES, 32, 128), BF16),
            vmem((LEAVES, 32, 128), BF16),
            vmem((LEAVES, 32, 128), BF16),
            vmem((LEAVES, 32, 128), BF16),
            vmem((64, 32, 128), BF16),
            vmem((LEAVES, COLS, 128), F32),
            vmem((LEAVES, COLS, 128), F32),
            vmem((64, 32, 128), F32),
            vmem((32, 32, 128), BF16),
            vmem((32, 32, 128), BF16),
            vmem((COLS, 128), BF16),
            vmem((COLS, 128), BF16),
            vmem((4, COLS, 128), BF16),
            vmem((32, COLS, 128), BF16),
            vmem((NRHS, LEAVES, COLS, WIDTH), F32),
            vmem((2, 16, COLS, WIDTH), F32),
            vmem((2, LEAVES, COLS, WIDTH), F32),
            dma((LEAVES,)),
            dma((9,)),
            dma((6,)),
            dma((6,)),
            dma((6,)),
            dma((6,)),
            dma((6,)),
            dma((6,)),
            dma((4,)),
            dma((4,)),
            dma((31,)),
            dma((31,)),
            dma((10,)),
            dma((10,)),
        ],
        compiler_params=pltpu.CompilerParams(
            collective_id=0, has_side_effects=True, vmem_limit_bytes=60 * 2**20
        ),
        name="h2_product",
    )(
        dens,
        bases,
        blocks,
        near_src.T,
        send_leaf.transpose(1, 2, 0),
        far_src.T,
        coupling,
        local_t[0].transpose(1, 2, 0).reshape(1024, 64),
        upper_t.transpose(1, 2, 0).reshape(1024, 128),
        up_c.transpose(1, 2, 3, 0).reshape(3, 1024, 128),
    )


def solution(mesh):
    in_specs = (
        P("rhs", "leaf"),
        P(None, "leaf"),
        P("leaf", "rhs", None, None),
        P("leaf", "rhs"),
        P(),
        P("leaf", None),
        P("leaf", None, None, None),
        P("leaf", None, None, None),
        P(),
        P(),
    )
    return jax.shard_map(
        local, mesh=mesh, in_specs=in_specs, out_specs=P("rhs", "leaf"), check_vma=False
    )
```

time: 46.6 us -> 38.2 us (0.82)
  the two profiles are of different devices: /device:TPU:32 before, /device:TPU:8 now
where the time goes in v3:
time: 38.2 us; the launch traced here: 38.1 us
  Pallas kernels  36.4 us (95%)
  local copies, waits for them, and re-layouts  1.67 us (4%)
    pallas_call x1, Pallas kernels, local(): pl.pallas_call(kernel, out_shape=jax.ShapeDtypeStruct((COLS, LEAVES * WID...  36.4 us
    unnamed x1, local copies, waits for them, and re-layouts  1.67 us

profile of v3, /device:TPU:8, one launch (start us, length us, event | category | flops | bytes accessed | tf_op | source)
XLA Modules:
  0.0 38.1 jit_solution(15911607141440952536)
XLA Ops:
  0.0 36.4 %h2_product.1 = f32[16,4096]{1,0:T(8,128)} custom-call(bf16[16,4096]{1,0:T(8,128)(2,1)} %dens.1, f32[32,4096]{1,0:T(8,128)} %bases.1, bf16[32,2,128,128]{3,2,1,0:T(8,128)(2,1)} %blocks.1, s32[2,32]{1,0:T(2,128)} %bitcast.19, s32[6,4,64]{2,1,0:T(4,128)} %bitcast.17, s32[8,32]{1,0:T(8,128)} %bitcast.18, f32[32,8,32,32]{3,2,1,0:T(8,128)} %coup.1, ...), custom_call_target="tpu_custom_call" | custom-call | tf_op jit(solution)/shard_map/h2_product/pallas_call | solution.py:540
  36.4 1.7 %copy.12 = f32[16,4096]{1,0:T(8,128)} copy(f32[16,4096]{1,0:T(8,128)} %h2_product.1) | data formatting | bytes 524288

commit v4 on v3

--- a/solution.py
+++ b/solution.py
@@ -17,7 +17,7 @@
 NRHS = 4
 SLOTS = 56
 FACES = (1, -1, 4, -4, 16, -16)
-GREET = (1, -1, 3, -3) + tuple(range(2, 64, 2))
+GREET = tuple(range(1, 9)) + (16, 24)
 
 
 def dot_nn(a, b):
@@ -128,6 +128,7 @@
     gr_sem,
     ps_sem,
     pr_sem,
+    news,
 ):
     d = lax.axis_index("leaf")
     me = lax.axis_index("rhs")
@@ -145,13 +146,32 @@
 
     my_rows = rows_of(me)
 
+    def inside(offset):
+        if offset > 0:
+            return d < NLEAF - offset
+        return d >= -offset
+
+    def greet(sem, offsets):
+        count = 0
+        for offset in offsets:
+            for o in (offset, -offset):
+                count = count + jnp.where(inside(o), 1, 0)
+
+                @pl.when(inside(o))
+                def _():
+                    pl.semaphore_signal(
+                        sem, inc=1, device_id={"leaf": d + o}, device_id_type=MESH
+                    )
+
+        return count
+
+    for k in range(LEAVES, SLOTS):
+        buf[k, my_rows, :] = jnp.zeros((COLS, WIDTH), BF16)
+
     barrier = pltpu.get_barrier_semaphore()
     for peer in (right, left):
         pl.semaphore_signal(barrier, inc=1, device_id={"rhs": peer}, device_id_type=MESH)
-    for offset in GREET:
-        pl.semaphore_signal(
-            barrier, inc=1, device_id={"leaf": leaf_at(offset)}, device_id_type=MESH
-        )
+    greeted = greet(barrier, GREET)
 
     def own_copy(k):
         return pltpu.make_async_copy(
@@ -201,6 +221,94 @@
             t_x[2 * p] = coef_form(jnp.concatenate([r[:, :32]] * 4, axis=1))
             t_x[2 * p + 1] = coef_form(jnp.concatenate([r[:, 32:]] * 4, axis=1))
 
+    @pl.loop(0, LEAVES)
+    def _(k):
+        own_copy(k).wait()
+
+    loads[2].wait()
+    for j in range(6):
+        for c in range(4):
+            wanted = jnp.maximum(sleaf[j, c, d], 0)
+            stage[j, c] = own[wanted]
+
+    @pl.loop(0, LEAVES, unroll=8)
+    def _(k):
+        buf[k, my_rows, :] = own[k]
+
+    pl.semaphore_wait(barrier, 2 + greeted)
+
+    near_planes = greet(news.at[0], (8, 16, 24))
+
+    side = 1 - 2 * lax.rem(d, 2)
+    third = d + 3 * side
+    third_ok = (third >= 0) & (third < NLEAF)
+    partners = (d + 2, d - 2, third, d + side)
+    root_out_ok = (inside(2), inside(-2), third_ok)
+    root_in_ok = (inside(-2), inside(2), third_ok)
+    root_sends = [
+        pltpu.make_async_remote_copy(
+            src_ref=root_x,
+            dst_ref=lrecv.at[i],
+            send_sem=ls_sem.at[i],
+            recv_sem=lr_sem.at[i],
+            device_id={"leaf": partner},
+            device_id_type=MESH,
+        )
+        for i, partner in enumerate(partners)
+    ]
+    halo_sends = [
+        pltpu.make_async_remote_copy(
+            src_ref=stage.at[j],
+            dst_ref=buf.at[pl.ds(LEAVES + 4 * j, 4), my_rows, :],
+            send_sem=hs_sem.at[j],
+            recv_sem=hr_sem.at[j],
+            device_id={"leaf": d + FACES[j]},
+            device_id_type=MESH,
+        )
+        for j in range(6)
+    ]
+
+    def over_rhs(src, dst, target, ssem, rsem):
+        return pltpu.make_async_remote_copy(
+            src_ref=src,
+            dst_ref=dst,
+            send_sem=ssem,
+            recv_sem=rsem,
+            device_id={"rhs": target},
+            device_id_type=MESH,
+        )
+
+    def pass_on(slots, target, source, index, ssem, rsem):
+        piece = buf.at[slots, rows_of(source), :]
+        return over_rhs(piece, piece, target, ssem.at[index], rsem.at[index])
+
+    lower, upper = pl.ds(0, 16), pl.ds(16, 16)
+    own_out = [
+        over_rhs(own.at[lower], buf.at[lower, my_rows, :], right, os_sem.at[0], or_sem.at[0]),
+        over_rhs(own.at[upper], buf.at[upper, my_rows, :], left, os_sem.at[1], or_sem.at[1]),
+        over_rhs(own.at[upper], buf.at[upper, my_rows, :], right, os_sem.at[2], or_sem.at[2]),
+        over_rhs(own.at[lower], buf.at[lower, my_rows, :], left, os_sem.at[3], or_sem.at[3]),
+    ]
+    own_relay = [
+        pass_on(lower, right, left, 4, os_sem, or_sem),
+        pass_on(upper, left, right, 5, os_sem, or_sem),
+    ]
+    first, second = pl.ds(LEAVES, 12), pl.ds(LEAVES + 12, 12)
+    halo_out = [
+        pass_on(first, right, me, 0, ys_sem, yr_sem),
+        pass_on(second, left, me, 1, ys_sem, yr_sem),
+        pass_on(second, right, me, 2, ys_sem, yr_sem),
+        pass_on(first, left, me, 3, ys_sem, yr_sem),
+    ]
+    halo_relay = [
+        pass_on(first, right, left, 4, ys_sem, yr_sem),
+        pass_on(second, left, right, 5, ys_sem, yr_sem),
+    ]
+    for j in range(6):
+        pl.when(inside(FACES[j]))(halo_sends[j].start)
+    for send in own_out:
+        send.start()
+
     loads[1].wait()
 
     @pl.loop(0, LEAVES, unroll=8)
@@ -212,10 +320,6 @@
         q_hi[t] = high
         q_lo[t] = low
 
-    @pl.loop(0, LEAVES)
-    def _(k):
-        own_copy(k).wait()
-
     root = jnp.zeros((COLS, 32), F32)
     for t in range(LEAVES):
         x = own[t]
@@ -223,83 +327,13 @@
             jnp.concatenate([x, x], axis=1), jnp.concatenate([q_hi[t], q_lo[t]], axis=1)
         )
     root_x[...] = coef_form(jnp.concatenate([root] * 4, axis=1))
-
-    loads[2].wait()
-    for j in range(6):
-        for c in range(4):
-            wanted = jnp.maximum(sleaf[j, c, d], 0)
-            stage[j, c] = own[wanted]
-
-    @pl.loop(0, LEAVES, unroll=8)
-    def _(k):
-        buf[k, my_rows, :] = own[k]
-
-    pl.semaphore_wait(barrier, 2 + len(GREET))
-
-    side = 1 - 2 * lax.rem(d, 2)
-    partners = (leaf_at(2), leaf_at(-2), lax.rem(d + 3 * side + NLEAF, NLEAF), d + side)
-    root_sends = [
-        pltpu.make_async_remote_copy(
-            src_ref=root_x,
-            dst_ref=lrecv.at[i],
-            send_sem=ls_sem.at[i],
-            recv_sem=lr_sem.at[i],
-            device_id={"leaf": partner},
-            device_id_type=MESH,
-        )
-        for i, partner in enumerate(partners)
-    ]
-    halo_sends = [
-        pltpu.make_async_remote_copy(
-            src_ref=stage.at[j],
-            dst_ref=buf.at[pl.ds(LEAVES + 4 * j, 4), my_rows, :],
-            send_sem=hs_sem.at[j],
-            recv_sem=hr_sem.at[j],
-            device_id={"leaf": leaf_at(FACES[j])},
-            device_id_type=MESH,
-        )
-        for j in range(6)
-    ]
-
-    def over_rhs(src, dst, target, ssem, rsem):
-        return pltpu.make_async_remote_copy(
-            src_ref=src,
-            dst_ref=dst,
-            send_sem=ssem,
-            recv_sem=rsem,
-            device_id={"rhs": target},
-            device_id_type=MESH,
-        )
-
-    def pass_on(slots, target, source, index, ssem, rsem):
-        piece = buf.at[slots, rows_of(source), :]
-        return over_rhs(piece, piece, target, ssem.at[index], rsem.at[index])
-
-    lower, upper = pl.ds(0, 16), pl.ds(16, 16)
-    own_out = [
-        over_rhs(own.at[lower], buf.at[lower, my_rows, :], right, os_sem.at[0], or_sem.at[0]),
-        over_rhs(own.at[upper], buf.at[upper, my_rows, :], left, os_sem.at[1], or_sem.at[1]),
-        over_rhs(own.at[upper], buf.at[upper, my_rows, :], right, os_sem.at[2], or_sem.at[2]),
-        over_rhs(own.at[lower], buf.at[lower, my_rows, :], left, os_sem.at[3], or_sem.at[3]),
-    ]
-    own_relay = [
-        pass_on(lower, right, left, 4, os_sem, or_sem),
-        pass_on(upper, left, right, 5, os_sem, or_sem),
-    ]
-    first, second = pl.ds(LEAVES, 12), pl.ds(LEAVES + 12, 12)
-    halo_out = [
-        pass_on(first, right, me, 0, ys_sem, yr_sem),
-        pass_on(second, left, me, 1, ys_sem, yr_sem),
-        pass_on(second, right, me, 2, ys_sem, yr_sem),
-        pass_on(first, left, me, 3, ys_sem, yr_sem),
-    ]
-    halo_relay = [
-        pass_on(first, right, left, 4, ys_sem, yr_sem),
-        pass_on(second, left, right, 5, ys_sem, yr_sem),
-    ]
     root_sends[3].start()
-    for send in own_out + halo_sends + root_sends[:3]:
-        send.start()
+    for i in range(3):
+        pl.when(root_out_ok[i])(root_sends[i].start)
+
+        @pl.when(jnp.logical_not(root_in_ok[i]))
+        def _():
+            lrecv[i] = jnp.zeros((COLS, 128), BF16)
 
     @pl.loop(0, LEAVES, unroll=8)
     def _(t):
@@ -308,6 +342,15 @@
         r = dot_nt(jnp.concatenate([x, x], axis=1), w)
         f_rep[t] = jnp.concatenate([r] * 4, axis=1)
 
+    for j in range(6):
+        pl.when(inside(-FACES[j]))(halo_sends[j].wait_recv)
+    for send in halo_out:
+        send.start()
+    for send in own_out[:2]:
+        send.wait_recv()
+    for send in own_relay:
+        send.start()
+
     loads[3].wait()
     for a in range(8):
         blk = jnp.concatenate([upt_v[pl.ds(32 * (8 * b + a), 32), :] for b in range(4)], axis=0)
@@ -320,7 +363,7 @@
     chip = lax.div(d, 2)
 
     def leaf_coupling(begin, count):
-        @pl.loop(begin, begin + count, unroll=4)
+        @pl.loop(begin, begin + count, unroll=8)
         def _(t):
             group = lane_group((COLS, 128))
             x_high, x_low, c_high, c_low = [], [], [], []
@@ -363,30 +406,21 @@
         )
         for k in range(1, 32)
     ]
-    for send in chip_sends:
-        send.start()
+    pl.semaphore_wait(news.at[0], near_planes)
+    far_planes = greet(news.at[1], (32,))
 
     loads[4].wait()
     loads[5].wait()
     leaf_coupling(0, 8)
-
-    for send in own_out[:2]:
-        send.wait_recv()
-    for send in own_relay:
-        send.start()
-    for send in halo_sends:
-        send.wait_recv()
-    for send in halo_out:
-        send.start()
-
-    leaf_coupling(8, 16)
 
     for send in halo_out[:2]:
         send.wait_recv()
     for send in halo_relay:
         send.start()
 
-    leaf_coupling(24, 8)
+    pl.semaphore_wait(news.at[1], far_planes)
+    for send in chip_sends:
+        send.start()
 
     loads[6].wait()
     loads[7].wait()
@@ -477,8 +511,12 @@
         elif level < 4:
             down = dot_nn(coef_form(down), rows_form(*halves(above(n))))
 
+    leaf_coupling(8, 8)
+
     join(2)
     join(3)
+
+    leaf_coupling(16, 16)
 
     for n in range(4, 8):
         m_rep[n] = jnp.zeros((32, 128), F32)
@@ -501,8 +539,8 @@
         m_hi[e] = high
         m_lo[e] = low
 
-    for send in root_sends[:3]:
-        send.wait_recv()
+    for i in range(3):
+        pl.when(root_in_ok[i])(root_sends[i].wait_recv)
     field = jnp.zeros((COLS, 128), F32)
     for c in range(3):
         field = field + dot_nn(lrecv[c], rows_form(*halves(couplings[0][c][1])))
@@ -516,18 +554,25 @@
         field = field + dot_nn(x, w)
     field_x = coef_form(field)
 
-    def finish(begin, count):
-        @pl.loop(begin, begin + count, unroll=8)
+    @pl.loop(0, LEAVES, unroll=8)
+    def _(t):
+        acc[t] = acc[t] + dot_nn(field_x, rows_form(q_hi[t], q_lo[t]))
+
+    for send in plain_sends:
+        send.wait_recv()
+    for i, begin in enumerate((0, 16, 8, 24)):
+        sum_sends[i].wait_recv()
+
+        @pl.loop(begin, begin + 8, unroll=8)
         def _(t):
-            far = acc[t] + dot_nn(field_x, rows_form(q_hi[t], q_lo[t]))
             near_sum = part[me, t] + (rbuf[0, t] + rbuf[1, t])
-            out[:, pl.ds(pl.multiple_of(t * WIDTH, WIDTH), WIDTH)] = near_sum + far
-
-    for send in plain_sends + sum_sends:
-        send.wait_recv()
-    finish(0, LEAVES)
-
-    for send in root_sends + halo_sends + own_out + own_relay + halo_out + halo_relay:
+            out[:, pl.ds(pl.multiple_of(t * WIDTH, WIDTH), WIDTH)] = near_sum + acc[t]
+
+    for j in range(6):
+        pl.when(inside(FACES[j]))(halo_sends[j].wait_send)
+    for i in range(3):
+        pl.when(root_out_ok[i])(root_sends[i].wait_send)
+    for send in root_sends[3:] + own_out + own_relay + halo_out + halo_relay:
         send.wait_send()
     for send in chip_sends + raw_sends + plain_sends + sum_sends:
         send.wait_send()
@@ -590,12 +635,16 @@
             dma((31,)),
             dma((10,)),
             dma((10,)),
+            pltpu.SemaphoreType.REGULAR((2,)),
         ],
         compiler_params=pltpu.CompilerParams(
-            collective_id=0, has_side_effects=True, vmem_limit_bytes=60 * 2**20
+            collective_id=0, has_side_effects=True, vmem_limit_bytes=48 * 2**20
         ),
         name="h2_product",
     )(
+        *(
+            pltpu.with_memory_space_constraint(x, pltpu.HBM)
+            for x in (
         dens,
         bases,
         blocks,
@@ -606,6 +655,8 @@
         local_t[0].transpose(1, 2, 0).reshape(1024, 64),
         upper_t.transpose(1, 2, 0).reshape(1024, 128),
         up_c.transpose(1, 2, 3, 0).reshape(3, 1024, 128),
+            )
+        )
     )
 
 

time: 38.2 us -> 34.3 us (0.90)
  the two profiles are of different devices: /device:TPU:8 before, /device:TPU:32 now
where the time goes in v4:
time: 34.3 us; the launch traced here: 34.2 us
  Pallas kernels  33.5 us (98%)
  local copies, waits for them, and re-layouts  0.71 us (2%)
    pallas_call x1, Pallas kernels, local(): pl.pallas_call(kernel, out_shape=jax.ShapeDtypeStruct((COLS, LEAVES * WID...  33.5 us
    unnamed x1, local copies, waits for them, and re-layouts  0.71 us

profile of v4, /device:TPU:32, one launch (start us, length us, event | category | flops | bytes accessed | tf_op | source)
XLA Modules:
  0.0 34.2 jit_solution(18073688509188256821)
XLA Ops:
  0.0 33.5 %h2_product.1 = f32[16,4096]{1,0:T(8,128)S(1)} custom-call(bf16[16,4096]{1,0:T(8,128)(2,1)} %dens.1, f32[32,4096]{1,0:T(8,128)} %bases.1, bf16[32,2,128,128]{3,2,1,0:T(8,128)(2,1)} %blocks.1, s32[2,32]{1,0:T(2,128)} %bitcast.19, s32[6,4,64]{2,1,0:T(4,128)} %bitcast.17, s32[8,32]{1,0:T(8,128)} %bitcast.18, f32[32,8,32,32]{3,2,1,0:T(8,128)} %coup.1, ...), custom_call_target="tpu_custom_call" | custom-call | tf_op jit(solution)/shard_map/h2_product/pallas_call | solution.py:585
  33.5 0.7 %copy.12 = f32[16,4096]{1,0:T(8,128)} copy(f32[16,4096]{1,0:T(8,128)S(1)} %h2_product.1) | data formatting | bytes 524288

commit v5 on v4

--- a/solution.py
+++ b/solution.py
@@ -103,6 +103,7 @@
     q_lo,
     t_x,
     f_rep,
+    ll_x,
     acc,
     m_rep,
     m_hi,
@@ -311,21 +312,30 @@
 
     loads[1].wait()
 
-    @pl.loop(0, LEAVES, unroll=8)
+    @pl.loop(0, LEAVES, step=2, unroll=4)
     def _(t):
-        high, low = halves(bas_v[:, pl.ds(pl.multiple_of(t * WIDTH, WIDTH), WIDTH)])
-        b_hi[t] = high
-        b_lo[t] = low
-        high, low = halves(dot_nn(t_x[LEAVES + t], rows_form(high, low)))
-        q_hi[t] = high
-        q_lo[t] = low
-
-    root = jnp.zeros((COLS, 32), F32)
-    for t in range(LEAVES):
-        x = own[t]
-        root = root + dot_nt(
-            jnp.concatenate([x, x], axis=1), jnp.concatenate([q_hi[t], q_lo[t]], axis=1)
-        )
+        maps = []
+        for k in range(2):
+            lanes = pl.ds(pl.multiple_of((t + k) * WIDTH, WIDTH), WIDTH)
+            b_hi[t + k], b_lo[t + k] = pair = halves(bas_v[:, lanes])
+            maps.append(rows_form(*pair))
+        x = jnp.concatenate([t_x[LEAVES + t], t_x[LEAVES + t + 1]], axis=0)
+        r = dot_nn(x, jnp.concatenate(maps, axis=1))
+        for k in range(2):
+            q_hi[t + k], q_lo[t + k] = halves(r[32 * k : 32 * k + 32, 128 * k : 128 * k + 128])
+
+    root = jnp.zeros((COLS, 64), F32)
+    for t in range(0, LEAVES, 2):
+        x = jnp.concatenate([own[t], own[t + 1]], axis=1)
+        w = jnp.concatenate(
+            [
+                jnp.concatenate([q_hi[t], q_hi[t + 1]], axis=1),
+                jnp.concatenate([q_lo[t], q_lo[t + 1]], axis=1),
+            ],
+            axis=0,
+        )
+        root = root + dot_nt(x, w)
+    root = root[:, :32] + root[:, 32:]
     root_x[...] = coef_form(jnp.concatenate([root] * 4, axis=1))
     root_sends[3].start()
     for i in range(3):
@@ -335,12 +345,16 @@
         def _():
             lrecv[i] = jnp.zeros((COLS, 128), BF16)
 
-    @pl.loop(0, LEAVES, unroll=8)
+    pl.semaphore_wait(news.at[0], near_planes)
+    far_planes = greet(news.at[1], (32,))
+
+    @pl.loop(0, LEAVES, step=4, unroll=4)
     def _(t):
-        w = jnp.concatenate([b_hi[t], b_lo[t]], axis=1)
-        x = own[t]
-        r = dot_nt(jnp.concatenate([x, x], axis=1), w)
-        f_rep[t] = jnp.concatenate([r] * 4, axis=1)
+        w = jnp.concatenate([m[t + k] for k in range(4) for m in (b_hi, b_lo)], axis=0)
+        r = dot_nt(jnp.concatenate([own[t + k] for k in range(4)], axis=0), w)
+        for k in range(4):
+            v = r[COLS * k : COLS * (k + 1), 64 * k : 64 * (k + 1)]
+            f_rep[t + k] = jnp.concatenate([v[:, :32] + v[:, 32:]] * 4, axis=1)
 
     for j in range(6):
         pl.when(inside(-FACES[j]))(halo_sends[j].wait_recv)
@@ -363,29 +377,30 @@
     chip = lax.div(d, 2)
 
     def leaf_coupling(begin, count):
-        @pl.loop(begin, begin + count, unroll=8)
+        @pl.loop(begin, begin + count, step=4, unroll=2)
         def _(t):
             group = lane_group((COLS, 128))
-            x_high, x_low, c_high, c_low = [], [], [], []
-            for half in range(2):
-                g = [f_rep[fsrc[4 * half + j, t]] for j in range(4)]
-                g = jnp.where(
-                    group < 2,
-                    jnp.where(group == 0, g[0], g[1]),
-                    jnp.where(group == 2, g[2], g[3]),
-                )
-                high, low = halves(g)
-                x_high.append(high)
-                x_low.append(low)
-                m = jnp.concatenate([cpl_v[t, 4 * half + j] for j in range(4)], axis=1)
-                high, low = halves(m)
-                c_high.append(high)
-                c_low.append(low)
-            x = jnp.concatenate(x_high + x_low + x_high, axis=1)
-            w = jnp.concatenate(c_high + c_high + c_low, axis=1)
-            r = dot_nt(x, w)
-            x = coef_form(jnp.concatenate([r] * 4, axis=1))
-            acc[t] = dot_nn(x, rows_form(b_hi[t], b_lo[t]))
+            xs, ws = [], []
+            for k in range(4):
+                x, w = [], []
+                for half in range(2):
+                    g = [f_rep[fsrc[4 * half + j, t + k]] for j in range(4)]
+                    g = jnp.where(
+                        group < 2,
+                        jnp.where(group == 0, g[0], g[1]),
+                        jnp.where(group == 2, g[2], g[3]),
+                    )
+                    x.append(halves(g))
+                    m = jnp.concatenate([cpl_v[t + k, 4 * half + j] for j in range(4)], axis=1)
+                    w.append(halves(m))
+                for part_of in range(2):
+                    xs.append(jnp.concatenate([v[part_of] for v in x], axis=1))
+                    ws.append(jnp.concatenate([v[part_of] for v in w], axis=1))
+            r = dot_nt(jnp.concatenate(xs, axis=0), jnp.concatenate(ws, axis=0))
+            for k in range(4):
+                v = r[32 * k : 32 * k + 32, 64 * k : 64 * k + 64]
+                v = v[:COLS] + v[COLS:]
+                ll_x[t + k] = coef_form(jnp.concatenate([v[:, :32] + v[:, 32:]] * 4, axis=1))
 
     root_sends[3].wait_recv()
     x = jnp.concatenate([root_x[...], lrecv[3]], axis=1)
@@ -406,8 +421,6 @@
         )
         for k in range(1, 32)
     ]
-    pl.semaphore_wait(news.at[0], near_planes)
-    far_planes = greet(news.at[1], (32,))
 
     loads[4].wait()
     loads[5].wait()
@@ -421,6 +434,8 @@
     pl.semaphore_wait(news.at[1], far_planes)
     for send in chip_sends:
         send.start()
+
+    leaf_coupling(8, 8)
 
     loads[6].wait()
     loads[7].wait()
@@ -511,12 +526,12 @@
         elif level < 4:
             down = dot_nn(coef_form(down), rows_form(*halves(above(n))))
 
-    leaf_coupling(8, 8)
+    leaf_coupling(16, 8)
 
     join(2)
     join(3)
 
-    leaf_coupling(16, 16)
+    leaf_coupling(24, 8)
 
     for n in range(4, 8):
         m_rep[n] = jnp.zeros((32, 128), F32)
@@ -554,9 +569,24 @@
         field = field + dot_nn(x, w)
     field_x = coef_form(field)
 
-    @pl.loop(0, LEAVES, unroll=8)
+    @pl.loop(0, LEAVES, step=2, unroll=4)
     def _(t):
-        acc[t] = acc[t] + dot_nn(field_x, rows_form(q_hi[t], q_lo[t]))
+        x = jnp.concatenate(
+            [jnp.concatenate([field_x, ll_x[t + k]], axis=1) for k in range(2)], axis=0
+        )
+        w = jnp.concatenate(
+            [
+                jnp.concatenate(
+                    [rows_form(q_hi[t + k], q_lo[t + k]), rows_form(b_hi[t + k], b_lo[t + k])],
+                    axis=0,
+                )
+                for k in range(2)
+            ],
+            axis=1,
+        )
+        r = dot_nn(x, w)
+        for k in range(2):
+            acc[t + k] = r[COLS * k : COLS * (k + 1), 128 * k : 128 * (k + 1)]
 
     for send in plain_sends:
         send.wait_recv()
@@ -610,6 +640,7 @@
             vmem((LEAVES, 32, 128), BF16),
             vmem((64, 32, 128), BF16),
             vmem((LEAVES, COLS, 128), F32),
+            vmem((LEAVES, COLS, 128), BF16),
             vmem((LEAVES, COLS, 128), F32),
             vmem((64, 32, 128), F32),
             vmem((32, 32, 128), BF16),

time: 34.3 us -> 31.2 us (0.910)
  Pallas kernels: 33.5 us -> 30.4 us
    pallas_call x1, Pallas kernels: 33.5 us -> 30.4 us  [local(): pl.pallas_call(kernel, out_shape=jax.ShapeDtypeStruct((COLS, LEAVES * WID...]
where the time goes in v5:
time: 31.2 us; the launch traced here: 31.1 us
  Pallas kernels  30.4 us (97%)
  local copies, waits for them, and re-layouts  0.71 us (2%)
    pallas_call x1, Pallas kernels, local(): pl.pallas_call(kernel, out_shape=jax.ShapeDtypeStruct((COLS, LEAVES * WID...  30.4 us
    unnamed x1, local copies, waits for them, and re-layouts  0.71 us

profile of v5, /device:TPU:32, one launch (start us, length us, event | category | flops | bytes accessed | tf_op | source)
XLA Modules:
  0.0 31.1 jit_solution(18182662310775347862)
XLA Ops:
  0.0 30.4 %h2_product.1 = f32[16,4096]{1,0:T(8,128)S(1)} custom-call(bf16[16,4096]{1,0:T(8,128)(2,1)} %dens.1, f32[32,4096]{1,0:T(8,128)} %bases.1, bf16[32,2,128,128]{3,2,1,0:T(8,128)(2,1)} %blocks.1, s32[2,32]{1,0:T(2,128)} %bitcast.19, s32[6,4,64]{2,1,0:T(4,128)} %bitcast.17, s32[8,32]{1,0:T(8,128)} %bitcast.18, f32[32,8,32,32]{3,2,1,0:T(8,128)} %coup.1, ...), custom_call_target="tpu_custom_call" | custom-call | tf_op jit(solution)/shard_map/h2_product/pallas_call | solution.py:615
  30.4 0.7 %copy.12 = f32[16,4096]{1,0:T(8,128)} copy(f32[16,4096]{1,0:T(8,128)S(1)} %h2_product.1) | data formatting | bytes 524288

commit v6 on v5

--- a/solution.py
+++ b/solution.py
@@ -17,6 +17,7 @@
 NRHS = 4
 SLOTS = 56
 FACES = (1, -1, 4, -4, 16, -16)
+VIA_RIGHT = (0, 3, 4)
 GREET = tuple(range(1, 9)) + (16, 24)
 
 
@@ -152,6 +153,10 @@
             return d < NLEAF - offset
         return d >= -offset
 
+    ends = (lax.rem(d, 4), lax.rem(lax.div(d, 4), 4), lax.div(d, 16))
+    face_out = [ends[j // 2] <= 2 if j % 2 == 0 else ends[j // 2] >= 1 for j in range(6)]
+    face_in = [face_out[j + 1 - 2 * (j % 2)] for j in range(6)]
+
     def greet(sem, offsets):
         count = 0
         for offset in offsets:
@@ -294,19 +299,19 @@
         pass_on(lower, right, left, 4, os_sem, or_sem),
         pass_on(upper, left, right, 5, os_sem, or_sem),
     ]
-    first, second = pl.ds(LEAVES, 12), pl.ds(LEAVES + 12, 12)
-    halo_out = [
-        pass_on(first, right, me, 0, ys_sem, yr_sem),
-        pass_on(second, left, me, 1, ys_sem, yr_sem),
-        pass_on(second, right, me, 2, ys_sem, yr_sem),
-        pass_on(first, left, me, 3, ys_sem, yr_sem),
-    ]
+    def face_on(j, target, source, index):
+        return pass_on(pl.ds(LEAVES + 4 * j, 4), target, source, index, ys_sem, yr_sem)
+
+    halo_right = [face_on(j, right, me, j) for j in range(6)]
+    halo_left = [face_on(j, left, me, 6 + j) for j in range(6)]
     halo_relay = [
-        pass_on(first, right, left, 4, ys_sem, yr_sem),
-        pass_on(second, left, right, 5, ys_sem, yr_sem),
-    ]
+        face_on(j, right, left, 12 + j) if j in VIA_RIGHT else face_on(j, left, right, 12 + j)
+        for j in range(6)
+    ]
+    halo_first = [halo_right[j] if j in VIA_RIGHT else halo_left[j] for j in range(6)]
+    halo_later = [halo_left[j] if j in VIA_RIGHT else halo_right[j] for j in range(6)]
     for j in range(6):
-        pl.when(inside(FACES[j]))(halo_sends[j].start)
+        pl.when(face_out[j])(halo_sends[j].start)
     for send in own_out:
         send.start()
 
@@ -357,9 +362,10 @@
             f_rep[t + k] = jnp.concatenate([v[:, :32] + v[:, 32:]] * 4, axis=1)
 
     for j in range(6):
-        pl.when(inside(-FACES[j]))(halo_sends[j].wait_recv)
-    for send in halo_out:
-        send.start()
+        pl.when(face_in[j])(halo_sends[j].wait_recv)
+    for group in (halo_first, halo_later):
+        for j in range(6):
+            pl.when(face_in[j])(group[j].start)
     for send in own_out[:2]:
         send.wait_recv()
     for send in own_relay:
@@ -426,10 +432,12 @@
     loads[5].wait()
     leaf_coupling(0, 8)
 
-    for send in halo_out[:2]:
-        send.wait_recv()
-    for send in halo_relay:
-        send.start()
+    for j in range(6):
+
+        @pl.when(face_in[j])
+        def _():
+            halo_first[j].wait_recv()
+            halo_relay[j].start()
 
     pl.semaphore_wait(news.at[1], far_planes)
     for send in chip_sends:
@@ -439,8 +447,14 @@
 
     loads[6].wait()
     loads[7].wait()
-    for send in own_out[2:] + own_relay + halo_out[2:] + halo_relay:
+    for send in own_out[2:] + own_relay:
         send.wait_recv()
+    for j in range(6):
+
+        @pl.when(face_in[j])
+        def _():
+            halo_later[j].wait_recv()
+            halo_relay[j].wait_recv()
 
     def near(begin, count):
         @pl.loop(begin, begin + count, unroll=8)
@@ -599,10 +613,16 @@
             out[:, pl.ds(pl.multiple_of(t * WIDTH, WIDTH), WIDTH)] = near_sum + acc[t]
 
     for j in range(6):
-        pl.when(inside(FACES[j]))(halo_sends[j].wait_send)
+        pl.when(face_out[j])(halo_sends[j].wait_send)
+
+        @pl.when(face_in[j])
+        def _():
+            for send in (halo_right[j], halo_left[j], halo_relay[j]):
+                send.wait_send()
+
     for i in range(3):
         pl.when(root_out_ok[i])(root_sends[i].wait_send)
-    for send in root_sends[3:] + own_out + own_relay + halo_out + halo_relay:
+    for send in root_sends[3:] + own_out + own_relay:
         send.wait_send()
     for send in chip_sends + raw_sends + plain_sends + sum_sends:
         send.wait_send()
@@ -658,8 +678,8 @@
             dma((6,)),
             dma((6,)),
             dma((6,)),
-            dma((6,)),
-            dma((6,)),
+            dma((18,)),
+            dma((18,)),
             dma((4,)),
             dma((4,)),
             dma((31,)),

time: 31.2 us -> 30.6 us (0.981)
  Pallas kernels: 30.4 us -> 29.6 us
    pallas_call x1, Pallas kernels: 30.4 us -> 29.6 us  [local(): pl.pallas_call(kernel, out_shape=jax.ShapeDtypeStruct((COLS, LEAVES * WID...]
where the time goes in v6:
time: 30.6 us; the launch traced here: 30.3 us
  Pallas kernels  29.6 us (97%)
  local copies, waits for them, and re-layouts  0.71 us (2%)
    pallas_call x1, Pallas kernels, local(): pl.pallas_call(kernel, out_shape=jax.ShapeDtypeStruct((COLS, LEAVES * WID...  29.6 us
    unnamed x1, local copies, waits for them, and re-layouts  0.71 us

profile of v6, /device:TPU:32, one launch (start us, length us, event | category | flops | bytes accessed | tf_op | source)
XLA Modules:
  0.0 30.3 jit_solution(12721452438377923236)
XLA Ops:
  0.0 29.6 %h2_product.1 = f32[16,4096]{1,0:T(8,128)S(1)} custom-call(bf16[16,4096]{1,0:T(8,128)(2,1)} %dens.1, f32[32,4096]{1,0:T(8,128)} %bases.1, bf16[32,2,128,128]{3,2,1,0:T(8,128)(2,1)} %blocks.1, s32[2,32]{1,0:T(2,128)} %bitcast.19, s32[6,4,64]{2,1,0:T(4,128)} %bitcast.17, s32[8,32]{1,0:T(8,128)} %bitcast.18, f32[32,8,32,32]{3,2,1,0:T(8,128)} %coup.1, ...), custom_call_target="tpu_custom_call" | custom-call | tf_op jit(solution)/shard_map/h2_product/pallas_call | solution.py:635
  29.6 0.7 %copy.12 = f32[16,4096]{1,0:T(8,128)} copy(f32[16,4096]{1,0:T(8,128)S(1)} %h2_product.1) | data formatting | bytes 524288
